TPU v7x, 512 devices: a whole 4x4x16 slice. The times are simulated.
512 devices in a mesh: runs: 64 (over x, z), tm: 8 (over y, core).
Axes of the slice: x: 4, y: 4, z: 16, core: 2. Of those that a mesh axis runs over, the one named last changes fastest.
Arguments:
- tensor: bfloat16 [1024, 128, 1024], P('runs', 'tm'), may hold values from 0 to 1
- run_counts: int32 [64], P('runs'), may hold values from 4 to 16, as said below
- run_init: float32 [1024, 128], P('runs'), may hold values from 0.05 to 0.5
- bin_init: float32 [1024, 128], replicated, may hold values from 0.05 to 0.5
- time_init: float32 [128, 128], P('tm'), may hold values from 0.05 to 0.5
Outputs:
- run_factor: float32 [1024, 128], P('runs')
- bin_factor: float32 [1024, 128], replicated
- time_factor: float32 [128, 128], P('tm')
Inputs may be any that keep to these rules, and one draw needn't show every extreme that they name: `run_counts`: at most 16 live slots on an index of runs; some index has exactly 16.
All inputs are finite; a program needn't handle non-finite values.
Results may differ from a plain program's by a relative error of at most 0.0003.
Values sent between devices are 32-bit elements; how exact they have to be, the bound alone decides.
No kernel may reach another device: no remote copies, remote signals or barrier semaphores. Data moves between devices by JAX's collectives and lax.ppermute only.
A program may use at most 64 MiB of HBM per device.

v0:
```python
import jax
import jax.numpy as jnp
from jax import lax
from jax.sharding import PartitionSpec as P

HIGH = lax.Precision.HIGHEST
STEP_ROWS = 8


def gram(factor):
    return jnp.dot(factor.T, factor, precision=HIGH)


def run_gram_sum(runs):
    return lax.psum(gram(runs), "runs")


def time_gram_sum(times):
    return lax.psum(gram(times), "tm")


def shards(tensor, run_counts, run_init, bin_init, time_init):
    rowcap = tensor.shape[0]
    count = run_counts[0]
    live = (jnp.arange(rowcap, dtype=jnp.int32) < count).astype(jnp.float32)[:, None]
    blocks = (count + STEP_ROWS - 1) // STEP_ROWS
    runs = run_init * live
    bins = bin_init
    times = time_init

    def sweep(step, init):
        return lax.fori_loop(0, blocks, lambda index, carry: step(index * STEP_ROWS, carry), init)

    run_gram = run_gram_sum(runs)
    bin_gram = gram(bins)
    time_gram = time_gram_sum(times)
    bins_low = bins.astype(jnp.bfloat16)

    def step(start, total):
        block = lax.dynamic_slice_in_dim(tensor, start, STEP_ROWS, 0)
        rows = lax.dynamic_slice_in_dim(runs, start, STEP_ROWS, 0)
        inner_sum = jnp.einsum("ikj,jr->ikr", block, bins_low, preferred_element_type=jnp.float32)
        return total + jnp.einsum("ir,ikr->kr", rows, inner_sum, precision=HIGH)

    local = sweep(step, jnp.zeros((tensor.shape[1], bins.shape[1]), jnp.float32))
    time_terms = lax.psum(local, "runs")
    times = times * time_terms / jnp.dot(times, run_gram * bin_gram, precision=HIGH)
    time_gram = time_gram_sum(times)
    times_low = times.astype(jnp.bfloat16)

    def step(start, total):
        block = lax.dynamic_slice_in_dim(tensor, start, STEP_ROWS, 0)
        rows = lax.dynamic_slice_in_dim(runs, start, STEP_ROWS, 0)
        partial_value = jnp.einsum(
            "ikj,kr->ijr", block, times_low, preferred_element_type=jnp.float32
        )
        return total + jnp.einsum("ir,ijr->jr", rows, partial_value, precision=HIGH)

    local_terms = sweep(step, jnp.zeros((tensor.shape[2], times.shape[1]), jnp.float32))
    mixing = run_gram * time_gram
    bin_terms = lax.psum(local_terms, ("runs", "tm"))
    bins = bins * bin_terms / jnp.dot(bins, mixing, precision=HIGH)
    bin_gram = gram(bins)
    run_bins_low = bins.astype(jnp.bfloat16)

    def step(start, total):
        block = lax.dynamic_slice_in_dim(tensor, start, STEP_ROWS, 0)
        inner_sum = jnp.einsum(
            "ikj,jr->ikr", block, run_bins_low, preferred_element_type=jnp.float32
        )
        row_terms = jnp.einsum("kr,ikr->ir", times, inner_sum, precision=HIGH)
        return lax.dynamic_update_slice_in_dim(total, row_terms, start, 0)

    local = sweep(step, jnp.zeros((rowcap, bins.shape[1]), jnp.float32))
    run_terms = lax.psum(local, "tm")
    runs = runs * run_terms / (jnp.dot(runs, bin_gram * time_gram, precision=HIGH) + 1.0 - live)
    return (runs, bins, times)


def solution(mesh):
    return jax.shard_map(
        shards,
        mesh=mesh,
        in_specs=(P("runs", "tm", None), P("runs"), P("runs", None), P(), P("tm", None)),
        out_specs=(P("runs", None), P(), P("tm", None)),
        check_vma=False,
    )
```

profile of v0, /device:TPU:1, one launch (start us, length us, event | category | flops | bytes accessed | tf_op | source)
XLA Modules:
  0.0 847.0 jit_solution(15681020974107471889)
XLA Ops:
  7.2 0.0 all-reduce.4.cloned.1.call-start
  7.9 0.8 broadcast_multiply_fusion
  8.7 0.9 fusion.20
  9.6 0.0 all-reduce.4.cloned.1.call-update
  9.6 0.0 all-reduce.8.cloned.1.call-start
  9.7 1.1 convert_element_type.17
  10.8 0.3 while.30
  10.9 0.2 fusion.45
  11.1 124.5 %psum.35 = f32[16,128]{1,0:T(8,128)S(1)} all-reduce(f32[16,128]{1,0:T(8,128)S(1)} %get-tuple-element.102), channel_id=1, replica_groups=mesh['runs'=64,'tm'=8] {'runs'}, use_global_device_ids=true, to_apply=%region_2.3 | all-reduce | flops 2048 | bytes 16384 | tf_op jit(solution)/shard_map/psum | solution.py:46
  135.7 133.1 %all-reduce.4.cloned.1.call-done = f32[128,128]{1,0:T(8,128)} async-done(((f32[128,128]{1,0:T(8,128)}), f32[128,128]{1,0:T(8,128)}) %all-reduce.4.cloned.1.call-update) | async-done | bytes 65552 | tf_op jit(solution)/shard_map/psum | solution.py:15
  268.8 1.8 convolution_multiply_fusion.1
  270.6 0.2 fusion.18
  270.8 0.9 fusion.21
  271.7 0.0 all-reduce.8.cloned.1.call-update
  271.7 0.0 all-reduce.6.cloned.1.call-start
  271.8 0.9 while.31
  271.9 0.8 multiply_reduce_fusion.2
  272.7 0.1 bitcast_add_fusion.5
  272.8 1.0 copy.8
  273.8 0.0 all-reduce.6.cloned.1.call-update
  273.8 0.2 copy.9
  274.0 76.4 %all-reduce.8.cloned.1.call-done = f32[128,128]{1,0:T(8,128)} async-done(((f32[128,128]{1,0:T(8,128)}), f32[128,128]{1,0:T(8,128)}) %all-reduce.8.cloned.1.call-update) | async-done | bytes 65552 | tf_op jit(solution)/shard_map/psum | solution.py:19
  350.4 471.4 %all-reduce.6.cloned.1.call-done = f32[1024,128]{0,1:T(8,128)} async-done(((f32[1024,128]{0,1:T(8,128)}), f32[1024,128]{0,1:T(8,128)}) %all-reduce.6.cloned.1.call-update) | async-done | bytes 524304 | tf_op jit(solution)/shard_map/psum | solution.py:61
  821.9 1.7 fusion.19
  823.6 1.0 copy.11
  824.6 0.2 copy.10
  824.8 0.3 while.32
  824.8 0.2 fusion.50
  825.1 0.0 copy-start.2
  825.1 14.0 %psum.39 = f32[16,128]{1,0:T(8,128)S(1)} all-reduce(f32[16,128]{1,0:T(8,128)S(1)} %get-tuple-element.104), channel_id=1, replica_groups=mesh['runs'=64,'tm'=8] {'tm'}, use_global_device_ids=true, to_apply=%region_10.11 | all-reduce | flops 2048 | bytes 16384 | tf_op jit(solution)/shard_map/psum | solution.py:75
  839.1 0.6 convolution_multiply_fusion
  839.7 0.8 fusion.15
  (19 shorter events, 0.1 us)
Async XLA Ops:
  7.2 3.6 copy-start
  7.2 261.6 %all-reduce.4.cloned.1.call-start = ((), (), s32[]{:S(2)}) async-start(), calls=%async_computation | async-start | bytes 131072 | tf_op jit(solution)/shard_map/psum | solution.py:15
  9.6 340.8 %all-reduce.8.cloned.1.call-start = ((), (), s32[]{:S(2)}) async-start(), calls=%async_computation.2 | async-start | bytes 131072 | tf_op jit(solution)/shard_map/psum | solution.py:19
  10.8 257.9 %copy-start.1 = (f32[1024,128]{1,0:T(8,128)S(1)}, f32[1024,128]{1,0:T(8,128)}, u32[]{:S(2)}) copy-start(f32[1024,128]{1,0:T(8,128)} %param.14) | copy-start | bytes 1572868
  135.6 135.0 %copy-start.5 = (f32[16,128]{1,0:T(8,128)S(1)}, f32[16,128]{1,0:T(8,128)}, u32[]{:S(2)}) copy-start(f32[16,128]{1,0:T(8,128)} %param.15) | copy-start | bytes 24580
  271.7 550.1 %all-reduce.6.cloned.1.call-start = ((), (), s32[]{:S(2)}) async-start(), calls=%async_computation.1 | async-start | bytes 1048576 | tf_op jit(solution)/shard_map/psum | solution.py:61
  273.8 548.0 %copy-start.3 = (f32[128,128]{1,0:T(8,128)S(1)}, f32[128,128]{1,0:T(8,128)}, u32[]{:S(2)}) copy-start(f32[128,128]{1,0:T(8,128)} %all-reduce.4.cloned.1.call-done) | copy-start | bytes 196612
  824.8 14.3 %copy-start.4 = (f32[128,128]{1,0:T(8,128)S(1)}, f32[128,128]{1,0:T(8,128)}, u32[]{:S(2)}) copy-start(f32[128,128]{1,0:T(8,128)} %all-reduce.8.cloned.1.call-done) | copy-start | bytes 196612
  825.1 14.6 %copy-start.2 = (f32[16,128]{1,0:T(8,128)}, f32[16,128]{1,0:T(8,128)S(1)}, u32[]{:S(2)}) copy-start(f32[16,128]{1,0:T(8,128)S(1)} %get-tuple-element.367) | copy-start | bytes 24580
Sparse Core Ops, SparseCore 0:
  12.0 256.7 all-reduce.3
  271.9 78.5 all-reduce.7
  356.5 465.3 all-reduce.5
where the time goes:
time: 847 us
  waiting for transfers between devices  681 us (80%)
  blocking collectives  138 us (16%)
  between operations  14.7 us (2%)
    psum x1, waiting for transfers between devices, shards(): bin_terms = lax.psum(local_terms, ('runs', 'tm'))  471 us
    psum x1, waiting for transfers between devices, run_gram_sum(): return lax.psum(gram(runs), 'runs')  133 us
    psum x1, blocking collectives, shards(): time_terms = lax.psum(local, 'runs')  125 us
    psum x1, waiting for transfers between devices, time_gram_sum(): return lax.psum(gram(times), 'tm')  76.4 us
  transfers between devices with their start and end apart: 3, of which 3 were waited for; matrix products, arithmetic and copies ran while one was open for 0% of the time, Pallas kernels for 0%

commit v1 on v0

v1 whole, which is shorter than its diff:
```python
import jax
import jax.numpy as jnp
from jax import lax
from jax.sharding import Mesh, PartitionSpec as P

HIGH = lax.Precision.HIGHEST
F32 = jnp.float32
BF16 = jnp.bfloat16
SIZES = {"x": 4, "z": 16, "y": 4, "c": 2}
PLANE = ("x", "y", "c")
TM = ("y", "c")


def gram(factor):
    return jnp.dot(factor.T, factor, precision=HIGH)


def extent(axes):
    total = 1
    for axis in axes:
        total *= SIZES[axis]
    return total


def exchange(parts, axes):
    return lax.all_to_all(parts, axes, 0, 0)


def spread(value, axes):
    copies = jnp.broadcast_to(value[None], (extent(axes),) + value.shape)
    return exchange(copies, axes)


def total(value, axes):
    return jnp.sum(spread(value, axes), axis=0)


def pieces(value):
    out = []
    for _ in range(3):
        part = lax.reduce_precision(value, 8, 7)
        out.append(part.astype(BF16))
        value = value - part
    return out


def shards(tensor, run_counts, run_init, bin_init, time_init):
    rowcap, rows, width = tensor.shape
    rank = run_init.shape[1]
    live = (jnp.arange(rowcap, dtype=jnp.int32) < run_counts[0]).astype(F32)[:, None]
    flat = tensor.reshape(rowcap * rows, width)
    runs = run_init * live
    bins_t = bin_init.T
    times = time_init

    run_gram = gram(runs)
    bin_gram = gram(bin_init)
    inner = jnp.dot(flat, bin_init.astype(BF16), preferred_element_type=F32)
    terms = jnp.sum(runs[:, None, :] * inner.reshape(rowcap, rows, rank), axis=0)
    below = jnp.dot(times, run_gram * bin_gram, precision=HIGH)
    both = jnp.concatenate([terms, below], axis=0)
    both = total(total(both, ("x",)), ("z",))
    times = times * both[:rows] / both[rows:]

    low = times.astype(BF16).astype(F32)
    weights = (runs[:, None, :] * low[None, :, :]).reshape(rowcap * rows, rank)
    terms = sum(
        lax.dot_general(part, flat, (((0,), (0,)), ((), ())), preferred_element_type=F32)
        for part in pieces(weights)
    )
    time_gram = gram(times)
    both = jnp.concatenate([terms, run_gram * time_gram], axis=1)
    count = extent(PLANE)
    chunk = rank // count
    both = jnp.sum(exchange(both.reshape(count, chunk, width + rank), PLANE), axis=0)
    both = total(both, ("z",))
    below = jnp.dot(both[:, width:], bins_t, precision=HIGH)
    mine = lax.dynamic_slice_in_dim(bins_t, lax.axis_index(PLANE) * chunk, chunk, 0)
    mine = mine * both[:, :width] / below
    bins_t = spread(mine, PLANE).reshape(rank, width)

    inner = lax.dot_general(
        flat, bins_t.astype(BF16), (((1,), (1,)), ((), ())), preferred_element_type=F32
    )
    terms = jnp.sum(times[None, :, :] * inner.reshape(rowcap, rows, rank), axis=1)
    bin_gram = jnp.dot(bins_t, bins_t.T, precision=HIGH)
    below = jnp.dot(runs, bin_gram * time_gram, precision=HIGH)
    both = total(jnp.concatenate([terms, below], axis=0), TM)
    runs = runs * both[:rowcap] / (both[rowcap:] + 1.0 - live)
    return (runs, bins_t.T, times)


def solution(mesh):
    fine = Mesh(mesh.devices.reshape(tuple(SIZES.values())), tuple(SIZES))
    return jax.shard_map(
        shards,
        mesh=fine,
        in_specs=(P(("x", "z"), TM, None), P(("x", "z")), P(("x", "z"), None), P(), P(TM, None)),
        out_specs=(P(("x", "z"), None), P(), P(TM, None)),
        check_vma=False,
    )
```

time: 847 us -> 122 us (0.14)
  waiting for transfers between devices: 681 us -> 19.8 us
  blocking collectives: 138 us -> 79.9 us
  between operations: 14.7 us -> 1.6 us
  starting transfers between devices: 0.12 us -> 8.61 us
    psum x3 -> x0, waiting for transfers between devices: 681 us -> none  [the longest x1 471 us: shards(): bin_terms = lax.psum(local_terms, ('runs', 'tm'))]
    psum x2 -> x0, blocking collectives: 138 us -> none  [the longest x1 125 us: shards(): time_terms = lax.psum(local, 'runs')]
    all_to_all x0 -> x4, blocking collectives: none -> 79.9 us  [exchange(): return lax.all_to_all(parts, axes, 0, 0)]
    all_to_all x0 -> x2, waiting for transfers between devices: none -> 19.8 us  [exchange(): return lax.all_to_all(parts, axes, 0, 0)]
    all_to_all x0 -> x2, starting transfers between devices: none -> 8.61 us  [exchange(): return lax.all_to_all(parts, axes, 0, 0)]
  transfers between devices with their start and end apart: 3 -> 2, of which waited for: 3 -> 2; matrix products, arithmetic and copies ran while one was open for 0% -> 1% of each run, Pallas kernels for 0% -> 0%
where the time goes in v1:
time: 122 us; the launch traced here: 121 us
  blocking collectives  79.9 us (65%)
  waiting for transfers between devices  19.8 us (16%)
  starting transfers between devices  8.61 us (7%)
  matrix products  5.67 us (5%)
  local copies, waits for them, and re-layouts  4.03 us (3%)
  other arithmetic  1.84 us (2%)
  between operations  1.6 us (1%)
    all_to_all x4, blocking collectives, exchange(): return lax.all_to_all(parts, axes, 0, 0)  79.9 us
    all_to_all x2, waiting for transfers between devices, exchange(): return lax.all_to_all(parts, axes, 0, 0)  19.8 us
    all_to_all x2, starting transfers between devices, exchange(): return lax.all_to_all(parts, axes, 0, 0)  8.61 us
    dot_general x3, matrix products, gram(): return jnp.dot(factor.T, factor, precision=HIGH)  2.85 us
  transfers between devices with their start and end apart: 2, of which 2 were waited for; matrix products, arithmetic and copies ran while one was open for 1% of the time, Pallas kernels for 0%

profile of v1, /device:TPU:1, one launch (start us, length us, event | category | flops | bytes accessed | tf_op | source)
XLA Modules:
  0.0 121.4 jit_solution(8574449804592550090)
XLA Ops:
  1.4 0.8 broadcast_multiply_fusion
  2.1 0.3 fusion.18
  2.4 2.3 %convolution_multiply_fusion.2 = f32[128,128]{0,1:T(8,128)S(1)} fusion(f32[128,128]{0,1:T(8,128)S(1)} %fusion.18, f32[1024,128]{1,0:T(8,128)} %param.8), kind=kOutput, calls=%fused_computation.9 | convolution fusion | flops 201342976 | bytes 655360 | tf_op jit(solution)/shard_map/dot_general | solution.py:15
  4.7 0.3 fusion.2
  5.0 0.4 copy-done.3
  5.4 0.2 convolution_bitcast_fusion.4
  5.7 9.1 %all_to_all.30 = f32[4,32,128]{2,1,0:T(8,128)S(1)} all-to-all(f32[4,32,128]{2,1,0:T(8,128)S(1)} %broadcast_in_dim.10), channel_id=1, replica_groups=mesh['x'=4,'z'=16,'y'=4,'c'=2] {'x'}, dimensions={0} | all-to-all | bytes 131072 | tf_op jit(solution)/shard_map/all_to_all | solution.py:26
  14.8 27.4 %all_to_all.31 = f32[16,32,128]{2,1,0:T(8,128)S(1)} all-to-all(f32[16,32,128]{2,1,0:T(8,128)S(1)} %broadcast_in_dim.11), channel_id=1, replica_groups=mesh['x'=4,'z'=16,'y'=4,'c'=2] {'z'}, dimensions={0} | all-to-all | bytes 524288 | tf_op jit(solution)/shard_map/all_to_all | solution.py:26
  42.3 0.3 convolution_bitcast_fusion
  42.6 0.3 convolution_bitcast_fusion.1
  42.8 0.3 fusion.17
  43.2 0.3 fusion.1
  43.5 0.2 reshape.41
  43.7 24.2 %all_to_all.32 = f32[32,4,1152]{2,1,0:T(4,128)S(1)} all-to-all(f32[32,4,1152]{2,1,0:T(4,128)S(1)} %reshape.41), channel_id=1, replica_groups=mesh['x'=4,'z'=16,'y'=4,'c'=2] {'x','y','c'}, dimensions={0} | all-to-all | bytes 1179648 | tf_op jit(solution)/shard_map/all_to_all | solution.py:26
  67.9 0.1 reduce_sum.66
  68.0 0.8 broadcast_in_dim.12
  68.8 5.3 %all-to-all-start.3 = ((f32[16,4,1152]{2,1,0:T(4,128)}), f32[16,4,1152]{2,1,0:T(4,128)S(1)}, u32[]{:S(2)}, u32[]{:S(2)}) async-start(f32[16,4,1152]{2,1,0:T(4,128)} %broadcast_in_dim.12), calls=%async_computation.3 | async-start | bytes 589824 | tf_op jit(solution)/shard_map/all_to_all | solution.py:26
  74.1 0.2 constant_dynamic-slice_fusion
  74.3 0.2 copy.32
  74.5 15.8 %all-to-all-done.3 = f32[16,4,1152]{2,1,0:T(4,128)S(1)} async-done(((f32[16,4,1152]{2,1,0:T(4,128)}), f32[16,4,1152]{2,1,0:T(4,128)S(1)}, u32[]{:S(2)}, u32[]{:S(2)}) %all-to-all-start.3) | async-done | bytes 294944 | tf_op jit(solution)/shard_map/all_to_all | solution.py:26
  90.4 0.5 convolution_divide_fusion
  90.9 0.1 broadcast_in_dim.13
  91.0 19.2 %all_to_all.33 = f32[32,4,1024]{2,1,0:T(4,128)S(1)} all-to-all(f32[32,4,1024]{2,1,0:T(4,128)S(1)} %broadcast_in_dim.13), channel_id=1, replica_groups=mesh['x'=4,'z'=16,'y'=4,'c'=2] {'x','y','c'}, dimensions={0} | all-to-all | bytes 1048576 | tf_op jit(solution)/shard_map/all_to_all | solution.py:26
  110.4 0.3 convolution_bitcast_fusion.3
  110.8 0.2 reshape.44
  111.0 0.6 convolution_multiply_fusion.1
  111.6 0.2 fusion.19
  111.8 0.7 broadcast_in_dim.14
  112.5 3.3 %all-to-all-start.5 = ((f32[8,32,128]{2,1,0:T(8,128)}), f32[8,32,128]{2,1,0:T(8,128)S(1)}, u32[]{:S(2)}, u32[]{:S(2)}) async-start(f32[8,32,128]{2,1,0:T(8,128)} %broadcast_in_dim.14), calls=%async_computation.5 | async-start | bytes 262144 | tf_op jit(solution)/shard_map/all_to_all | solution.py:26
  115.8 1.0 copy.28
  116.8 3.9 %all-to-all-done.5 = f32[8,32,128]{2,1,0:T(8,128)S(1)} async-done(((f32[8,32,128]{2,1,0:T(8,128)}), f32[8,32,128]{2,1,0:T(8,128)S(1)}, u32[]{:S(2)}, u32[]{:S(2)}) %all-to-all-start.5) | async-done | bytes 131104 | tf_op jit(solution)/shard_map/all_to_all | solution.py:26
  120.8 0.7 fusion.15
  (25 shorter events, 0.6 us)
Async XLA Ops:
  0.6 4.1 %copy-start = (bf16[16,16,1024]{2,1,0:T(8,128)(2,1)S(1)}, bf16[16,16,1024]{2,1,0:T(8,128)(2,1)}, u32[]{:S(2)}) copy-start(bf16[16,16,1024]{2,1,0:T(8,128)(2,1)} %param.5) | copy-start | bytes 1572868
  2.4 2.3 %copy-start.1 = (f32[1024,128]{1,0:T(8,128)S(1)}, f32[1024,128]{1,0:T(8,128)}, u32[]{:S(2)}) copy-start(f32[1024,128]{1,0:T(8,128)} %param.8) | copy-start | bytes 1572868
  4.7 0.7 copy-start.3
  42.3 68.5 %copy-start.2 = (f32[16,128]{1,0:T(8,128)}, f32[16,128]{1,0:T(8,128)S(1)}, u32[]{:S(2)}) copy-start(f32[16,128]{1,0:T(8,128)S(1)} %get-tuple-element.13) | copy-start | bytes 24580
  68.8 21.5 %all-to-all-start.3 = ((f32[16,4,1152]{2,1,0:T(4,128)}), f32[16,4,1152]{2,1,0:T(4,128)S(1)}, u32[]{:S(2)}, u32[]{:S(2)}) async-start(f32[16,4,1152]{2,1,0:T(4,128)} %broadcast_in_dim.12), calls=%async_computation.3 | async-start | bytes 589824 | tf_op jit(solution)/shard_map/all_to_all | solution.py:26
  112.5 8.3 %all-to-all-start.5 = ((f32[8,32,128]{2,1,0:T(8,128)}), f32[8,32,128]{2,1,0:T(8,128)S(1)}, u32[]{:S(2)}, u32[]{:S(2)}) async-start(f32[8,32,128]{2,1,0:T(8,128)} %broadcast_in_dim.14), calls=%async_computation.5 | async-start | bytes 262144 | tf_op jit(solution)/shard_map/all_to_all | solution.py:26
  116.8 3.9 %copy-start.4 = (f32[16,128]{1,0:T(8,128)S(1)}, f32[16,128]{1,0:T(8,128)}, u32[]{:S(2)}) copy-start(f32[16,128]{1,0:T(8,128)} %param.7) | copy-start | bytes 24580

commit v2 on v1

--- a/solution.py
+++ b/solution.py
@@ -6,8 +6,11 @@
 HIGH = lax.Precision.HIGHEST
 F32 = jnp.float32
 BF16 = jnp.bfloat16
-SIZES = {"x": 4, "z": 16, "y": 4, "c": 2}
-PLANE = ("x", "y", "c")
+SIZES = {"x": 4, "h": 8, "l": 2, "y": 4, "c": 2}
+RUNS = ("x", "h", "l")
+NEAR = ("x", "l")
+FAR = ("h",)
+PLANE = ("x", "l", "y", "c")
 TM = ("y", "c")
 
 
@@ -59,10 +62,10 @@
     terms = jnp.sum(runs[:, None, :] * inner.reshape(rowcap, rows, rank), axis=0)
     below = jnp.dot(times, run_gram * bin_gram, precision=HIGH)
     both = jnp.concatenate([terms, below], axis=0)
-    both = total(total(both, ("x",)), ("z",))
+    both = total(total(both, NEAR), FAR)
     times = times * both[:rows] / both[rows:]
 
-    low = times.astype(BF16).astype(F32)
+    low = lax.reduce_precision(times, 8, 7)
     weights = (runs[:, None, :] * low[None, :, :]).reshape(rowcap * rows, rank)
     terms = sum(
         lax.dot_general(part, flat, (((0,), (0,)), ((), ())), preferred_element_type=F32)
@@ -73,7 +76,7 @@
     count = extent(PLANE)
     chunk = rank // count
     both = jnp.sum(exchange(both.reshape(count, chunk, width + rank), PLANE), axis=0)
-    both = total(both, ("z",))
+    both = total(both, FAR)
     below = jnp.dot(both[:, width:], bins_t, precision=HIGH)
     mine = lax.dynamic_slice_in_dim(bins_t, lax.axis_index(PLANE) * chunk, chunk, 0)
     mine = mine * both[:, :width] / below
@@ -95,7 +98,7 @@
     return jax.shard_map(
         shards,
         mesh=fine,
-        in_specs=(P(("x", "z"), TM, None), P(("x", "z")), P(("x", "z"), None), P(), P(TM, None)),
-        out_specs=(P(("x", "z"), None), P(), P(TM, None)),
+        in_specs=(P(RUNS, TM, None), P(RUNS), P(RUNS, None), P(), P(TM, None)),
+        out_specs=(P(RUNS, None), P(), P(TM, None)),
         check_vma=False,
     )

time: 122 us -> 116 us (0.951)
  waiting for transfers between devices: 19.8 us -> 16.1 us
  starting transfers between devices: 8.61 us -> 7.1 us
    all_to_all x2, waiting for transfers between devices: 19.8 us -> 16.1 us  [exchange(): return lax.all_to_all(parts, axes, 0, 0)]
    all_to_all x2, starting transfers between devices: 8.61 us -> 7.1 us  [exchange(): return lax.all_to_all(parts, axes, 0, 0)]
where the time goes in v2:
time: 116 us
  blocking collectives  78.8 us (68%)
  waiting for transfers between devices  16.1 us (14%)
  starting transfers between devices  7.1 us (6%)
  matrix products  5.67 us (5%)
  local copies, waits for them, and re-layouts  4.34 us (4%)
  other arithmetic  2 us (2%)
  between operations  1.6 us (1%)
    all_to_all x4, blocking collectives, exchange(): return lax.all_to_all(parts, axes, 0, 0)  78.8 us
    all_to_all x2, waiting for transfers between devices, exchange(): return lax.all_to_all(parts, axes, 0, 0)  16.1 us
    all_to_all x2, starting transfers between devices, exchange(): return lax.all_to_all(parts, axes, 0, 0)  7.1 us
    dot_general x3, matrix products, gram(): return jnp.dot(factor.T, factor, precision=HIGH)  2.85 us
  transfers between devices with their start and end apart: 2, of which 2 were waited for; matrix products, arithmetic and copies ran while one was open for 1% of the time, Pallas kernels for 0%

profile of v2, /device:TPU:1, one launch (start us, length us, event | category | flops | bytes accessed | tf_op | source)
XLA Modules:
  0.0 115.6 jit_solution(8119519853369527118)
XLA Ops:
  1.4 0.8 broadcast_multiply_fusion
  2.1 0.3 fusion.19
  2.4 2.3 %convolution_multiply_fusion.2 = f32[128,128]{0,1:T(8,128)S(1)} fusion(f32[128,128]{0,1:T(8,128)S(1)} %fusion.19, f32[1024,128]{1,0:T(8,128)} %param.8), kind=kOutput, calls=%fused_computation.9 | convolution fusion | flops 201342976 | bytes 655360 | tf_op jit(solution)/shard_map/dot_general | solution.py:18
  4.7 0.3 fusion.2
  5.0 0.4 copy-done.3
  5.4 0.2 convolution_bitcast_fusion.4
  5.7 11.5 %all_to_all.30 = f32[8,32,128]{2,1,0:T(8,128)S(1)} all-to-all(f32[8,32,128]{2,1,0:T(8,128)S(1)} %broadcast_in_dim.10), channel_id=1, replica_groups=mesh['x'=4,'h'=8,'l'=2,'y'=4,'c'=2] {'x','l'}, dimensions={0} | all-to-all | bytes 262144 | tf_op jit(solution)/shard_map/all_to_all | solution.py:29
  17.2 27.0 %all_to_all.31 = f32[8,32,128]{2,1,0:T(8,128)S(1)} all-to-all(f32[8,32,128]{2,1,0:T(8,128)S(1)} %broadcast_in_dim.11), channel_id=1, replica_groups=mesh['x'=4,'h'=8,'l'=2,'y'=4,'c'=2] {'h'}, dimensions={0} | all-to-all | bytes 262144 | tf_op jit(solution)/shard_map/all_to_all | solution.py:29
  44.2 0.3 convolution_bitcast_fusion
  44.5 0.3 convolution_bitcast_fusion.1
  44.8 0.3 fusion.18
  45.2 0.3 fusion.1
  45.5 0.3 reshape.41
  45.8 22.0 %all_to_all.32 = f32[64,2,1152]{2,1,0:T(2,128)S(1)} all-to-all(f32[64,2,1152]{2,1,0:T(2,128)S(1)} %reshape.41), channel_id=1, replica_groups=mesh['x'=4,'h'=8,'l'=2,'y'=4,'c'=2] {'x','l','y','c'}, dimensions={0} | all-to-all | bytes 1179648 | tf_op jit(solution)/shard_map/all_to_all | solution.py:29
  67.8 0.2 reduce_sum.66
  68.0 0.7 broadcast_in_dim.12
  68.7 3.4 %all-to-all-start.3 = ((f32[8,2,1152]{2,1,0:T(2,128)}), f32[8,2,1152]{2,1,0:T(2,128)S(1)}, u32[]{:S(2)}, u32[]{:S(2)}) async-start(f32[8,2,1152]{2,1,0:T(2,128)} %broadcast_in_dim.12), calls=%async_computation.3 | async-start | bytes 147456 | tf_op jit(solution)/shard_map/all_to_all | solution.py:29
  72.0 0.2 constant_dynamic-slice_fusion
  72.2 0.2 copy.32
  72.4 11.8 %all-to-all-done.3 = f32[8,2,1152]{2,1,0:T(2,128)S(1)} async-done(((f32[8,2,1152]{2,1,0:T(2,128)}), f32[8,2,1152]{2,1,0:T(2,128)S(1)}, u32[]{:S(2)}, u32[]{:S(2)}) %all-to-all-start.3) | async-done | bytes 73760 | tf_op jit(solution)/shard_map/all_to_all | solution.py:29
  84.3 0.5 convolution_divide_fusion
  84.9 18.3 %all_to_all.33 = f32[64,2,1024]{2,1,0:T(2,128)S(1)} all-to-all(f32[64,2,1024]{2,1,0:T(2,128)S(1)} %broadcast_in_dim.13), channel_id=1, replica_groups=mesh['x'=4,'h'=8,'l'=2,'y'=4,'c'=2] {'x','l','y','c'}, dimensions={0} | all-to-all | bytes 1048576 | tf_op jit(solution)/shard_map/all_to_all | solution.py:29
  103.3 0.2 convert_element_type.33
  103.5 0.3 convolution_bitcast_fusion.3
  104.0 0.4 reshape.44
  104.4 0.6 convolution_multiply_fusion.1
  105.0 0.2 fusion.20
  105.2 0.7 broadcast_in_dim.14
  105.8 3.7 %all-to-all-start.5 = ((f32[8,32,128]{2,1,0:T(8,128)}), f32[8,32,128]{2,1,0:T(8,128)S(1)}, u32[]{:S(2)}, u32[]{:S(2)}) async-start(f32[8,32,128]{2,1,0:T(8,128)} %broadcast_in_dim.14), calls=%async_computation.5 | async-start | bytes 262144 | tf_op jit(solution)/shard_map/all_to_all | solution.py:29
  109.6 1.0 copy.28
  110.6 4.3 %all-to-all-done.5 = f32[8,32,128]{2,1,0:T(8,128)S(1)} async-done(((f32[8,32,128]{2,1,0:T(8,128)}), f32[8,32,128]{2,1,0:T(8,128)S(1)}, u32[]{:S(2)}, u32[]{:S(2)}) %all-to-all-start.5) | async-done | bytes 131104 | tf_op jit(solution)/shard_map/all_to_all | solution.py:29
  114.9 0.7 fusion.15
  (25 shorter events, 0.7 us)
Async XLA Ops:
  0.6 4.1 %copy-start = (bf16[16,16,1024]{2,1,0:T(8,128)(2,1)S(1)}, bf16[16,16,1024]{2,1,0:T(8,128)(2,1)}, u32[]{:S(2)}) copy-start(bf16[16,16,1024]{2,1,0:T(8,128)(2,1)} %param.5) | copy-start | bytes 1572868
  2.4 2.3 %copy-start.1 = (f32[1024,128]{1,0:T(8,128)S(1)}, f32[1024,128]{1,0:T(8,128)}, u32[]{:S(2)}) copy-start(f32[1024,128]{1,0:T(8,128)} %param.8) | copy-start | bytes 1572868
  4.7 0.7 copy-start.3
  44.2 59.7 %copy-start.2 = (f32[16,128]{1,0:T(8,128)}, f32[16,128]{1,0:T(8,128)S(1)}, u32[]{:S(2)}) copy-start(f32[16,128]{1,0:T(8,128)S(1)} %get-tuple-element.13) | copy-start | bytes 24580
  68.7 15.6 %all-to-all-start.3 = ((f32[8,2,1152]{2,1,0:T(2,128)}), f32[8,2,1152]{2,1,0:T(2,128)S(1)}, u32[]{:S(2)}, u32[]{:S(2)}) async-start(f32[8,2,1152]{2,1,0:T(2,128)} %broadcast_in_dim.12), calls=%async_computation.3 | async-start | bytes 147456 | tf_op jit(solution)/shard_map/all_to_all | solution.py:29
  105.8 9.0 %all-to-all-start.5 = ((f32[8,32,128]{2,1,0:T(8,128)}), f32[8,32,128]{2,1,0:T(8,128)S(1)}, u32[]{:S(2)}, u32[]{:S(2)}) async-start(f32[8,32,128]{2,1,0:T(8,128)} %broadcast_in_dim.14), calls=%async_computation.5 | async-start | bytes 262144 | tf_op jit(solution)/shard_map/all_to_all | solution.py:29
  110.6 4.3 %copy-start.4 = (f32[16,128]{1,0:T(8,128)S(1)}, f32[16,128]{1,0:T(8,128)}, u32[]{:S(2)}) copy-start(f32[16,128]{1,0:T(8,128)} %param.7) | copy-start | bytes 24580

commit v3 on v2

v3 whole, which is shorter than its diff:
```python
import jax
import jax.numpy as jnp
from jax import lax
from jax.experimental import pallas as pl
from jax.experimental.pallas import tpu as pltpu
from jax.sharding import Mesh, PartitionSpec as P

HIGH = lax.Precision.HIGHEST
F32 = jnp.float32
BF16 = jnp.bfloat16
SIZES = {"x": 4, "h": 8, "l": 2, "y": 4, "c": 2}
RUNS = ("x", "h", "l")
NEAR = ("x", "l")
FAR = ("h",)
PLANE = ("x", "l", "y", "c")
TM = ("y", "c")
FIRST = (((0,), (0,)), ((), ()))
LAST = (((1,), (1,)), ((), ()))


def exact(left, right, dims):
    return lax.dot_general(left, right, dims, precision=HIGH, preferred_element_type=F32)


def quick(left, right, dims):
    return lax.dot_general(left, right, dims, preferred_element_type=F32)


def extent(axes):
    total = 1
    for axis in axes:
        total *= SIZES[axis]
    return total


def exchange(parts, axes):
    return lax.all_to_all(parts, axes, 0, 0)


def added(parts):
    total = parts[0]
    for part in range(1, parts.shape[0]):
        total += parts[part]
    return total


def terms_kernel(count, index, *refs):
    far, (both, runs_out, gram_out, pick, *near), sems = refs[:4], refs[4:12], refs[12]
    tensor, bins, run_init, times = near
    copies = [pltpu.make_async_copy(far[i], near[i], sems.at[i]) for i in range(4)]
    for copy in reversed(copies):
        copy.start()
    rowcap, rank = run_init.shape
    rows = times.shape[0]
    chunk = pick.shape[0]
    row = lax.broadcasted_iota(jnp.int32, (chunk, rank), 0) + index[0] * chunk
    column = lax.broadcasted_iota(jnp.int32, (chunk, rank), 1)
    pick[...] = jnp.where(column == row, 1.0, 0.0)
    slot = lax.broadcasted_iota(jnp.int32, (rowcap, rank), 0)
    copies[2].wait()
    copies[3].wait()
    runs = jnp.where(slot < count[0], run_init[...], 0.0)
    runs_out[...] = runs
    run_gram = exact(runs, runs, FIRST)
    gram_out[...] = run_gram
    copies[1].wait()
    full = bins[...]
    below = jnp.dot(times[...], run_gram * exact(full, full, FIRST), precision=HIGH)
    copies[0].wait()
    inner = jnp.dot(tensor[...], full.astype(BF16), preferred_element_type=F32)
    terms = runs[0:1] * inner[0:rows]
    for i in range(1, rowcap):
        terms += runs[i : i + 1] * inner[i * rows : (i + 1) * rows]
    for copy in range(both.shape[0]):
        both[copy, 0:rows] = terms
        both[copy, rows:] = below


def time_kernel(parts, times, runs, run_gram, tensor, out, times_out, gram_out):
    rows, rank = times.shape
    rowcap = runs.shape[0]
    width = tensor.shape[1]
    sums = added(parts)
    new = times[...] * sums[:rows] / sums[rows:]
    times_out[...] = new
    time_gram = exact(new, new, FIRST)
    gram_out[...] = time_gram
    low = new.astype(BF16).astype(F32)
    left = jnp.concatenate([runs[i : i + 1] * low for i in range(rowcap)], axis=0)
    block = tensor[...]
    terms = None
    for _ in range(3):
        part = left.astype(BF16)
        term = quick(part, block, FIRST)
        terms = term if terms is None else terms + term
        left = left - part.astype(F32)
    out[:, :, 0:width] = terms.reshape(out.shape[0], out.shape[1], width)
    mixing = run_gram[...] * time_gram
    out[:, :, width:] = mixing.reshape(out.shape[0], out.shape[1], rank)


def spread_kernel(parts, out):
    total = added(parts)
    for copy in range(out.shape[0]):
        out[copy] = total


def bins_kernel(parts, bins, pick, out):
    count, chunk, width = out.shape
    sums = added(parts)
    left = jnp.concatenate([sums[:, width:], pick[...]], axis=0)
    got = exact(left, bins[...], LAST)
    mine = got[chunk:] * sums[:, :width] / got[:chunk]
    for copy in range(count):
        out[copy] = mine


def runs_kernel(parts, tensor, runs, times, time_gram, both, bins_out):
    rank, width = bins_out.shape
    rowcap = runs.shape[0]
    rows = times.shape[0]
    bins = parts[...].reshape(rank, width)
    bins_out[...] = bins
    inner = quick(tensor[...], bins.astype(BF16), LAST)
    mixing = exact(bins, bins, LAST) * time_gram[...]
    below = jnp.dot(runs[...], mixing, precision=HIGH)
    for copy in range(both.shape[0]):
        both[copy, rowcap:] = below
    for i in range(rowcap):
        term = jnp.sum(times[...] * inner[i * rows : (i + 1) * rows], axis=0, keepdims=True)
        for copy in range(both.shape[0]):
            both[copy, i : i + 1] = term


def last_kernel(count, parts, runs, out):
    rowcap, rank = runs.shape
    sums = added(parts)
    slot = lax.broadcasted_iota(jnp.int32, (rowcap, rank), 0)
    empty = jnp.where(slot < count[0], 0.0, 1.0)
    out[...] = runs[...] * sums[:rowcap] / (sums[rowcap:] + empty)


def local(kernel, scalars, arrays, shapes, space=pltpu.VMEM, **more):
    near = pl.BlockSpec(memory_space=pltpu.VMEM)
    if space is pltpu.VMEM:
        arrays = [pltpu.with_memory_space_constraint(array, space) for array in arrays]
    return pl.pallas_call(
        kernel,
        out_shape=tuple(
            shape if hasattr(shape, "dtype") else pltpu.VMEM(shape, F32) for shape in shapes
        ),
        in_specs=[pl.BlockSpec(memory_space=pltpu.SMEM)] * len(scalars)
        + [pl.BlockSpec(memory_space=space)] * len(arrays),
        out_specs=(near,) * len(shapes),
        **more,
    )(*scalars, *arrays)


def shards(tensor, run_counts, run_init, bin_init, time_init):
    rowcap, rows, width = tensor.shape
    rank = run_init.shape[1]
    flat = tensor.reshape(rowcap * rows, width)
    plane = extent(PLANE)
    chunk = rank // plane
    index = lax.axis_index(PLANE).reshape(1)

    both, runs, run_gram, pick, flat, bins, _, times = local(
        terms_kernel,
        (run_counts, index),
        (flat, bin_init, run_init, time_init),
        (
            (extent(NEAR), 2 * rows, rank),
            (rowcap, rank),
            (rank, rank),
            (chunk, rank),
            pltpu.VMEM(flat.shape, flat.dtype),
            bin_init.shape,
            (rowcap, rank),
            (rows, rank),
        ),
        pl.ANY,
        scratch_shapes=[pltpu.SemaphoreType.DMA((4,))],
    )
    both = jnp.sum(exchange(both, NEAR), axis=0)
    both = exchange(jnp.broadcast_to(both[None], (extent(FAR),) + both.shape), FAR)
    both, times, time_gram = local(
        time_kernel,
        (),
        (both, times, runs, run_gram, flat),
        ((plane, chunk, width + rank), (rows, rank), (rank, rank)),
    )
    both = exchange(both, PLANE)
    (both,) = local(spread_kernel, (), (both,), ((extent(FAR), chunk, width + rank),))
    both = exchange(both, FAR)
    (mine,) = local(bins_kernel, (), (both, bins, pick), ((plane, chunk, width),))
    both, bins = local(
        runs_kernel,
        (),
        (exchange(mine, PLANE), flat, runs, times, time_gram),
        ((extent(TM), 2 * rowcap, rank), (rank, width)),
    )
    both = exchange(both, TM)
    result = jax.ShapeDtypeStruct((rowcap, rank), F32)
    (runs,) = local(last_kernel, (run_counts,), (both, runs), (result,))
    return (runs, bins.T, times)


def solution(mesh):
    fine = Mesh(mesh.devices.reshape(tuple(SIZES.values())), tuple(SIZES))
    return jax.shard_map(
        shards,
        mesh=fine,
        in_specs=(P(RUNS, TM, None), P(RUNS), P(RUNS, None), P(), P(TM, None)),
        out_specs=(P(RUNS, None), P(), P(TM, None)),
        check_vma=False,
    )
```

time: 116 us -> 111 us (0.957)
  blocking collectives: 78.8 us -> 94 us
  waiting for transfers between devices: 16.1 us -> 3.67 us
  Pallas kernels: 0 us -> 6.16 us
  matrix products: 5.67 us -> 0 us
  starting transfers between devices: 7.1 us -> 3.75 us
  local copies, waits for them, and re-layouts: 4.34 us -> 1.6 us
  other arithmetic: 2 us -> 0.01 us
    all_to_all x4 -> x5, blocking collectives: 78.8 us -> 94 us  [exchange(): return lax.all_to_all(parts, axes, 0, 0)]
    all_to_all x2 -> x1, waiting for transfers between devices: 16.1 us -> 3.67 us  [exchange(): return lax.all_to_all(parts, axes, 0, 0)]
    pallas_call x0 -> x6, Pallas kernels: none -> 6.16 us  [local(): pl.pallas_call(kernel, out_shape=tuple((shape if hasattr(shape, 'dtype')...]
    dot_general x12 -> x0, matrix products: 5.67 us -> none  [the longest x3 2.85 us: gram(): return jnp.dot(factor.T, factor, precision=HIGH)]
    all_to_all x2 -> x1, starting transfers between devices: 7.1 us -> 3.75 us  [exchange(): return lax.all_to_all(parts, axes, 0, 0)]
    broadcast_in_dim x5 -> x1, local copies, waits for them, and re-layouts: 1.55 us -> 0.01 us  [shards(): jnp.broadcast_to(both[None], (extent(FAR),) + both.shape)]
  transfers between devices with their start and end apart: 2 -> 1, of which waited for: 2 -> 1; matrix products, arithmetic and copies ran while one was open for 1% -> 1% of each run, Pallas kernels for 0% -> 0%
where the time goes in v3:
time: 111 us
  blocking collectives  94 us (85%)
  Pallas kernels  6.16 us (6%)
  starting transfers between devices  3.75 us (3%)
  waiting for transfers between devices  3.67 us (3%)
  local copies, waits for them, and re-layouts  1.6 us (1%)
  between operations  1.32 us (1%)
    all_to_all x5, blocking collectives, exchange(): return lax.all_to_all(parts, axes, 0, 0)  94 us
    pallas_call x6, Pallas kernels, local(): pl.pallas_call(kernel, out_shape=tuple((shape if hasattr(shape, 'dtype')...  6.16 us
    all_to_all x1, starting transfers between devices, exchange(): return lax.all_to_all(parts, axes, 0, 0)  3.75 us
    all_to_all x1, waiting for transfers between devices, exchange(): return lax.all_to_all(parts, axes, 0, 0)  3.67 us
  transfers between devices with their start and end apart: 1, of which 1 were waited for; matrix products, arithmetic and copies ran while one was open for 1% of the time, Pallas kernels for 0%

profile of v3, /device:TPU:1, one launch (start us, length us, event | category | flops | bytes accessed | tf_op | source)
XLA Modules:
  0.0 110.5 jit_solution(7433467457399405444)
XLA Ops:
  1.3 2.8 %shard_map.76 = (f32[8,32,128]{2,1,0:T(8,128)S(1)}, f32[16,128]{1,0:T(8,128)S(1)}, f32[128,128]{1,0:T(8,128)S(1)}, f32[2,128]{1,0:T(2,128)S(1)}, bf16[256,1024]{...) custom-call(s32[1]{0:T(128)S(6)} %copy.10.count, s32[1]{0:T(128)} %bitcast.index, ...), custom_call_target="tpu_custom_call" | custom-call | tf_op jit(solution)/shard_map/pallas_call | solution.py:147
  4.1 11.5 %all_to_all.30 = f32[8,32,128]{2,1,0:T(8,128)S(1)} all-to-all(f32[8,32,128]{2,1,0:T(8,128)S(1)} %get-tuple-element.15), channel_id=1, replica_groups=mesh['x'=4,'h'=8,'l'=2,'y'=4,'c'=2] {'x','l'}, dimensions={0} | all-to-all | bytes 262144 | tf_op jit(solution)/shard_map/all_to_all | solution.py:37
  15.7 27.0 %all_to_all.31.parts = f32[8,32,128]{2,1,0:T(8,128)S(1)} all-to-all(f32[8,32,128]{2,1,0:T(8,128)S(1)} %broadcast_in_dim.2), channel_id=1, replica_groups=mesh['x'=4,'h'=8,'l'=2,'y'=4,'c'=2] {'h'}, dimensions={0} | all-to-all | bytes 262144 | tf_op jit(solution)/shard_map/all_to_all | solution.py:37
  42.6 0.5 shard_map.77
  43.1 22.0 %all_to_all.32.parts = f32[64,2,1152]{2,1,0:T(2,128)S(1)} all-to-all(f32[64,2,1152]{2,1,0:T(2,128)S(1)} %get-tuple-element.20), channel_id=1, replica_groups=mesh['x'=4,'h'=8,'l'=2,'y'=4,'c'=2] {'x','l','y','c'}, dimensions={0} | all-to-all | bytes 1179648 | tf_op jit(solution)/shard_map/all_to_all | solution.py:37
  65.1 0.1 shard_map.78
  65.2 15.0 %all_to_all.33.parts = f32[8,2,1152]{2,1,0:T(2,128)S(1)} all-to-all(f32[8,2,1152]{2,1,0:T(2,128)S(1)} %shard_map.78), channel_id=1, replica_groups=mesh['x'=4,'h'=8,'l'=2,'y'=4,'c'=2] {'h'}, dimensions={0} | all-to-all | bytes 147456 | tf_op jit(solution)/shard_map/all_to_all | solution.py:37
  80.2 0.6 shard_map.79
  80.8 18.5 %all_to_all.34.parts = f32[64,2,1024]{2,1,0:T(2,128)S(1)} all-to-all(f32[64,2,1024]{2,1,0:T(2,128)S(1)} %shard_map.79), channel_id=1, replica_groups=mesh['x'=4,'h'=8,'l'=2,'y'=4,'c'=2] {'x','l','y','c'}, dimensions={0} | all-to-all | bytes 1048576 | tf_op jit(solution)/shard_map/all_to_all | solution.py:37
  99.3 1.6 %shard_map.80 = (f32[8,32,128]{2,1,0:T(8,128)}, f32[128,1024]{1,0:T(8,128)S(1)}) custom-call(f32[64,2,1024]{2,1,0:T(2,128)S(1)} %all_to_all.34.parts, bf16[256,1024]{1,0:T(8,128)(2,1)S(1)} %get-tuple-element.19.tensor, f32[16,128]{1,0:T(8,128)S(1)} %get-tuple-element.17.runs, f32[16,128]{1,0:T(8,128)S(1)} %get-tuple-element.32.times, ...), custom_call_target="tpu_custom_call" | custom-call | tf_op jit(solution)/shard_map/pallas_call | solution.py:147
  100.9 3.8 %all-to-all-start.5 = ((f32[8,32,128]{2,1,0:T(8,128)}), f32[8,32,128]{2,1,0:T(8,128)S(1)}, u32[]{:S(2)}, u32[]{:S(2)}) async-start(f32[8,32,128]{2,1,0:T(8,128)} %get-tuple-element.25), calls=%async_computation.5 | async-start | bytes 262144 | tf_op jit(solution)/shard_map/all_to_all | solution.py:37
  104.6 0.6 copy.9
  105.2 1.0 copy.8
  106.2 3.7 %all-to-all-done.5.parts = f32[8,32,128]{2,1,0:T(8,128)S(1)} async-done(((f32[8,32,128]{2,1,0:T(8,128)}), f32[8,32,128]{2,1,0:T(8,128)S(1)}, u32[]{:S(2)}, u32[]{:S(2)}) %all-to-all-start.5) | async-done | bytes 131104 | tf_op jit(solution)/shard_map/all_to_all | solution.py:37
  109.9 0.6 shard_map.81
  (2 shorter events, 0.0 us)
Async XLA Ops:
  100.9 9.0 %all-to-all-start.5 = ((f32[8,32,128]{2,1,0:T(8,128)}), f32[8,32,128]{2,1,0:T(8,128)S(1)}, u32[]{:S(2)}, u32[]{:S(2)}) async-start(f32[8,32,128]{2,1,0:T(8,128)} %get-tuple-element.25), calls=%async_computation.5 | async-start | bytes 262144 | tf_op jit(solution)/shard_map/all_to_all | solution.py:37

commit v4 on v3

--- a/solution.py
+++ b/solution.py
@@ -8,6 +8,7 @@
 HIGH = lax.Precision.HIGHEST
 F32 = jnp.float32
 BF16 = jnp.bfloat16
+BLOCKS = 4
 SIZES = {"x": 4, "h": 8, "l": 2, "y": 4, "c": 2}
 RUNS = ("x", "h", "l")
 NEAR = ("x", "l")
@@ -44,36 +45,55 @@
     return total
 
 
-def terms_kernel(count, index, *refs):
-    far, (both, runs_out, gram_out, pick, *near), sems = refs[:4], refs[4:12], refs[12]
+def terms_kernel(*refs):
+    far, (both, runs_out, gram_out, pick, empty, *near), (number, sems) = refs[:5], refs[5:14], refs[14:]
     tensor, bins, run_init, times = near
-    copies = [pltpu.make_async_copy(far[i], near[i], sems.at[i]) for i in range(4)]
-    for copy in reversed(copies):
-        copy.start()
     rowcap, rank = run_init.shape
     rows = times.shape[0]
     chunk = pick.shape[0]
-    row = lax.broadcasted_iota(jnp.int32, (chunk, rank), 0) + index[0] * chunk
+    block = tensor.shape[0] // BLOCKS
+
+    def part(i):
+        return pl.ds(i * block, block)
+
+    count_copy = pltpu.make_async_copy(far[4], number, sems.at[0])
+    small = [pltpu.make_async_copy(far[i], near[i], sems.at[i]) for i in (2, 3)]
+    bins_copy = pltpu.make_async_copy(far[1], bins, sems.at[1])
+    large = [
+        pltpu.make_async_copy(far[0].at[part(i)], tensor.at[part(i)], sems.at[4 + i])
+        for i in range(BLOCKS)
+    ]
+    for copy in [count_copy, *small, bins_copy, *large]:
+        copy.start()
+    row = lax.broadcasted_iota(jnp.int32, (chunk, rank), 0) + lax.axis_index(PLANE) * chunk
     column = lax.broadcasted_iota(jnp.int32, (chunk, rank), 1)
     pick[...] = jnp.where(column == row, 1.0, 0.0)
+    count_copy.wait()
+    for copy in small:
+        copy.wait()
     slot = lax.broadcasted_iota(jnp.int32, (rowcap, rank), 0)
-    copies[2].wait()
-    copies[3].wait()
-    runs = jnp.where(slot < count[0], run_init[...], 0.0)
+    live = slot < number[0]
+    empty[...] = jnp.where(live, 0.0, 1.0)
+    runs = jnp.where(live, run_init[...], 0.0)
     runs_out[...] = runs
     run_gram = exact(runs, runs, FIRST)
     gram_out[...] = run_gram
-    copies[1].wait()
+    bins_copy.wait()
     full = bins[...]
     below = jnp.dot(times[...], run_gram * exact(full, full, FIRST), precision=HIGH)
-    copies[0].wait()
-    inner = jnp.dot(tensor[...], full.astype(BF16), preferred_element_type=F32)
-    terms = runs[0:1] * inner[0:rows]
-    for i in range(1, rowcap):
-        terms += runs[i : i + 1] * inner[i * rows : (i + 1) * rows]
+    low = full.astype(BF16)
+    for copy in range(both.shape[0]):
+        both[copy, rows:] = below
+    terms = None
+    for i in range(BLOCKS):
+        large[i].wait()
+        inner = jnp.dot(tensor[part(i)], low, preferred_element_type=F32)
+        for j in range(block // rows):
+            slot = i * (block // rows) + j
+            term = runs[slot : slot + 1] * inner[j * rows : (j + 1) * rows]
+            terms = term if terms is None else terms + term
     for copy in range(both.shape[0]):
         both[copy, 0:rows] = terms
-        both[copy, rows:] = below
 
 
 def time_kernel(parts, times, runs, run_gram, tensor, out, times_out, gram_out):
@@ -132,16 +152,13 @@
             both[copy, i : i + 1] = term
 
 
-def last_kernel(count, parts, runs, out):
-    rowcap, rank = runs.shape
+def last_kernel(parts, runs, empty, out):
+    rowcap = runs.shape[0]
     sums = added(parts)
-    slot = lax.broadcasted_iota(jnp.int32, (rowcap, rank), 0)
-    empty = jnp.where(slot < count[0], 0.0, 1.0)
-    out[...] = runs[...] * sums[:rowcap] / (sums[rowcap:] + empty)
-
-
-def local(kernel, scalars, arrays, shapes, space=pltpu.VMEM, **more):
-    near = pl.BlockSpec(memory_space=pltpu.VMEM)
+    out[...] = runs[...] * sums[:rowcap] / (sums[rowcap:] + empty[...])
+
+
+def local(kernel, arrays, shapes, space=pltpu.VMEM, **more):
     if space is pltpu.VMEM:
         arrays = [pltpu.with_memory_space_constraint(array, space) for array in arrays]
     return pl.pallas_call(
@@ -149,11 +166,10 @@
         out_shape=tuple(
             shape if hasattr(shape, "dtype") else pltpu.VMEM(shape, F32) for shape in shapes
         ),
-        in_specs=[pl.BlockSpec(memory_space=pltpu.SMEM)] * len(scalars)
-        + [pl.BlockSpec(memory_space=space)] * len(arrays),
-        out_specs=(near,) * len(shapes),
+        in_specs=[pl.BlockSpec(memory_space=space)] * len(arrays),
+        out_specs=(pl.BlockSpec(memory_space=pltpu.VMEM),) * len(shapes),
         **more,
-    )(*scalars, *arrays)
+    )(*arrays)
 
 
 def shards(tensor, run_counts, run_init, bin_init, time_init):
@@ -162,46 +178,43 @@
     flat = tensor.reshape(rowcap * rows, width)
     plane = extent(PLANE)
     chunk = rank // plane
-    index = lax.axis_index(PLANE).reshape(1)
-
-    both, runs, run_gram, pick, flat, bins, _, times = local(
+
+    both, runs, run_gram, pick, empty, flat, bins, _, times = local(
         terms_kernel,
-        (run_counts, index),
-        (flat, bin_init, run_init, time_init),
+        (flat, bin_init, run_init, time_init, run_counts),
         (
             (extent(NEAR), 2 * rows, rank),
             (rowcap, rank),
             (rank, rank),
             (chunk, rank),
+            (rowcap, rank),
             pltpu.VMEM(flat.shape, flat.dtype),
             bin_init.shape,
             (rowcap, rank),
             (rows, rank),
         ),
         pl.ANY,
-        scratch_shapes=[pltpu.SemaphoreType.DMA((4,))],
+        scratch_shapes=[pltpu.SMEM((1,), jnp.int32), pltpu.SemaphoreType.DMA((4 + BLOCKS,))],
     )
     both = jnp.sum(exchange(both, NEAR), axis=0)
     both = exchange(jnp.broadcast_to(both[None], (extent(FAR),) + both.shape), FAR)
     both, times, time_gram = local(
         time_kernel,
-        (),
         (both, times, runs, run_gram, flat),
         ((plane, chunk, width + rank), (rows, rank), (rank, rank)),
     )
     both = exchange(both, PLANE)
-    (both,) = local(spread_kernel, (), (both,), ((extent(FAR), chunk, width + rank),))
+    (both,) = local(spread_kernel, (both,), ((extent(FAR), chunk, width + rank),))
     both = exchange(both, FAR)
-    (mine,) = local(bins_kernel, (), (both, bins, pick), ((plane, chunk, width),))
+    (mine,) = local(bins_kernel, (both, bins, pick), ((plane, chunk, width),))
     both, bins = local(
         runs_kernel,
-        (),
         (exchange(mine, PLANE), flat, runs, times, time_gram),
         ((extent(TM), 2 * rowcap, rank), (rank, width)),
     )
     both = exchange(both, TM)
     result = jax.ShapeDtypeStruct((rowcap, rank), F32)
-    (runs,) = local(last_kernel, (run_counts,), (both, runs), (result,))
+    (runs,) = local(last_kernel, (both, runs, empty), (result,))
     return (runs, bins.T, times)
 
 

time: 111 us -> 111 us (level)
  no operation moved by 1% of the time
where the time goes in v4:
time: 111 us
  blocking collectives  94 us (85%)
  Pallas kernels  6.58 us (6%)
  starting transfers between devices  3.74 us (3%)
  waiting for transfers between devices  3.67 us (3%)
  local copies, waits for them, and re-layouts  1.6 us (1%)
  between operations  1.31 us (1%)
    all_to_all x5, blocking collectives, exchange(): return lax.all_to_all(parts, axes, 0, 0)  94 us
    pallas_call x6, Pallas kernels, local(): pl.pallas_call(kernel, out_shape=tuple((shape if hasattr(shape, 'dtype')...  6.58 us
    all_to_all x1, starting transfers between devices, exchange(): return lax.all_to_all(parts, axes, 0, 0)  3.74 us
    all_to_all x1, waiting for transfers between devices, exchange(): return lax.all_to_all(parts, axes, 0, 0)  3.67 us
  transfers between devices with their start and end apart: 1, of which 1 were waited for; matrix products, arithmetic and copies ran while one was open for 1% of the time, Pallas kernels for 0%

profile of v4, /device:TPU:1, one launch (start us, length us, event | category | flops | bytes accessed | tf_op | source)
XLA Modules:
  0.0 110.9 jit_solution(10641871287768475348)
XLA Ops:
  1.3 3.2 %shard_map.76 = (f32[8,32,128]{2,1,0:T(8,128)S(1)}, f32[16,128]{1,0:T(8,128)S(1)}, f32[128,128]{1,0:T(8,128)S(1)}, f32[2,128]{1,0:T(2,128)S(1)}, f32[16,128]{1,0...) custom-call(bf16[256,1024]{1,0:T(8,128)(2,1)} %bitcast.3, ...), custom_call_target="tpu_custom_call" | custom-call | tf_op jit(solution)/shard_map/pallas_call | solution.py:164
  4.5 11.5 %all_to_all.30 = f32[8,32,128]{2,1,0:T(8,128)S(1)} all-to-all(f32[8,32,128]{2,1,0:T(8,128)S(1)} %get-tuple-element.16), channel_id=1, replica_groups=mesh['x'=4,'h'=8,'l'=2,'y'=4,'c'=2] {'x','l'}, dimensions={0} | all-to-all | bytes 262144 | tf_op jit(solution)/shard_map/all_to_all | solution.py:38
  16.0 27.0 %all_to_all.31.parts = f32[8,32,128]{2,1,0:T(8,128)S(1)} all-to-all(f32[8,32,128]{2,1,0:T(8,128)S(1)} %broadcast_in_dim.2), channel_id=1, replica_groups=mesh['x'=4,'h'=8,'l'=2,'y'=4,'c'=2] {'h'}, dimensions={0} | all-to-all | bytes 262144 | tf_op jit(solution)/shard_map/all_to_all | solution.py:38
  43.0 0.5 shard_map.77
  43.5 22.0 %all_to_all.32.parts = f32[64,2,1152]{2,1,0:T(2,128)S(1)} all-to-all(f32[64,2,1152]{2,1,0:T(2,128)S(1)} %get-tuple-element.21), channel_id=1, replica_groups=mesh['x'=4,'h'=8,'l'=2,'y'=4,'c'=2] {'x','l','y','c'}, dimensions={0} | all-to-all | bytes 1179648 | tf_op jit(solution)/shard_map/all_to_all | solution.py:38
  65.5 0.1 shard_map.78
  65.6 15.0 %all_to_all.33.parts = f32[8,2,1152]{2,1,0:T(2,128)S(1)} all-to-all(f32[8,2,1152]{2,1,0:T(2,128)S(1)} %shard_map.78), channel_id=1, replica_groups=mesh['x'=4,'h'=8,'l'=2,'y'=4,'c'=2] {'h'}, dimensions={0} | all-to-all | bytes 147456 | tf_op jit(solution)/shard_map/all_to_all | solution.py:38
  80.6 0.6 shard_map.79
  81.2 18.5 %all_to_all.34.parts = f32[64,2,1024]{2,1,0:T(2,128)S(1)} all-to-all(f32[64,2,1024]{2,1,0:T(2,128)S(1)} %shard_map.79), channel_id=1, replica_groups=mesh['x'=4,'h'=8,'l'=2,'y'=4,'c'=2] {'x','l','y','c'}, dimensions={0} | all-to-all | bytes 1048576 | tf_op jit(solution)/shard_map/all_to_all | solution.py:38
  99.6 1.6 %shard_map.80 = (f32[8,32,128]{2,1,0:T(8,128)}, f32[128,1024]{1,0:T(8,128)S(1)}) custom-call(f32[64,2,1024]{2,1,0:T(2,128)S(1)} %all_to_all.34.parts, bf16[256,1024]{1,0:T(8,128)(2,1)S(1)} %get-tuple-element.20.tensor, f32[16,128]{1,0:T(8,128)S(1)} %get-tuple-element.18.runs, f32[16,128]{1,0:T(8,128)S(1)} %get-tuple-element.34.times, ...), custom_call_target="tpu_custom_call" | custom-call | tf_op jit(solution)/shard_map/pallas_call | solution.py:164
  101.3 3.7 %all-to-all-start.5 = ((f32[8,32,128]{2,1,0:T(8,128)}), f32[8,32,128]{2,1,0:T(8,128)S(1)}, u32[]{:S(2)}, u32[]{:S(2)}) async-start(f32[8,32,128]{2,1,0:T(8,128)} %get-tuple-element.26), calls=%async_computation.5 | async-start | bytes 262144 | tf_op jit(solution)/shard_map/all_to_all | solution.py:38
  105.0 0.6 copy.9
  105.6 1.0 copy.8
  106.6 3.7 %all-to-all-done.5.parts = f32[8,32,128]{2,1,0:T(8,128)S(1)} async-done(((f32[8,32,128]{2,1,0:T(8,128)}), f32[8,32,128]{2,1,0:T(8,128)S(1)}, u32[]{:S(2)}, u32[]{:S(2)}) %all-to-all-start.5) | async-done | bytes 131104 | tf_op jit(solution)/shard_map/all_to_all | solution.py:38
  110.3 0.6 shard_map.81
  (2 shorter events, 0.0 us)
Async XLA Ops:
  101.3 9.0 %all-to-all-start.5 = ((f32[8,32,128]{2,1,0:T(8,128)}), f32[8,32,128]{2,1,0:T(8,128)S(1)}, u32[]{:S(2)}, u32[]{:S(2)}) async-start(f32[8,32,128]{2,1,0:T(8,128)} %get-tuple-element.26), calls=%async_computation.5 | async-start | bytes 262144 | tf_op jit(solution)/shard_map/all_to_all | solution.py:38

commit v5 on v3

--- a/solution.py
+++ b/solution.py
@@ -12,7 +12,8 @@
 RUNS = ("x", "h", "l")
 NEAR = ("x", "l")
 FAR = ("h",)
-PLANE = ("x", "l", "y", "c")
+PLANE = ("x", "l", "y")
+PAIR = ("c",)
 TM = ("y", "c")
 FIRST = (((0,), (0,)), ((), ()))
 LAST = (((1,), (1,)), ((), ()))
@@ -35,6 +36,10 @@
 
 def exchange(parts, axes):
     return lax.all_to_all(parts, axes, 0, 0)
+
+
+def swap(value):
+    return lax.ppermute(value, PAIR, [(0, 1), (1, 0)])
 
 
 def added(parts):
@@ -53,7 +58,7 @@
     rowcap, rank = run_init.shape
     rows = times.shape[0]
     chunk = pick.shape[0]
-    row = lax.broadcasted_iota(jnp.int32, (chunk, rank), 0) + index[0] * chunk
+    row = lax.broadcasted_iota(jnp.int32, (chunk, rank), 0) + index[0]
     column = lax.broadcasted_iota(jnp.int32, (chunk, rank), 1)
     pick[...] = jnp.where(column == row, 1.0, 0.0)
     slot = lax.broadcasted_iota(jnp.int32, (rowcap, rank), 0)
@@ -76,7 +81,7 @@
         both[copy, rows:] = below
 
 
-def time_kernel(parts, times, runs, run_gram, tensor, out, times_out, gram_out):
+def time_kernel(parts, times, runs, run_gram, tensor, own, other, times_out, gram_out, whole):
     rows, rank = times.shape
     rowcap = runs.shape[0]
     width = tensor.shape[1]
@@ -94,9 +99,16 @@
         term = quick(part, block, FIRST)
         terms = term if terms is None else terms + term
         left = left - part.astype(F32)
-    out[:, :, 0:width] = terms.reshape(out.shape[0], out.shape[1], width)
-    mixing = run_gram[...] * time_gram
-    out[:, :, width:] = mixing.reshape(out.shape[0], out.shape[1], rank)
+    whole[:, 0:width] = terms
+    whole[:, width:] = run_gram[...] * time_gram
+    half = own.shape[0]
+    core = lax.axis_index(PAIR)
+    own[...] = whole[pl.ds(core * half, half)]
+    other[...] = whole[pl.ds((1 - core) * half, half)]
+
+
+def pair_kernel(own, other, out):
+    out[...] = (own[...] + other[...]).reshape(out.shape)
 
 
 def spread_kernel(parts, out):
@@ -115,21 +127,45 @@
         out[copy] = mine
 
 
-def runs_kernel(parts, tensor, runs, times, time_gram, both, bins_out):
-    rank, width = bins_out.shape
+def half_kernel(parts, tensor, times, bins_out, terms_out):
+    half, width = bins_out.shape
+    rows = times.shape[0]
+    core = lax.axis_index(PAIR)
+    bins = parts[...].reshape(half, width)
+    bins_out[...] = bins
+    inner = quick(tensor[...], bins.astype(BF16), LAST)
+    both = times[...]
+    mine = jnp.where(core == 0, both[:, :half], both[:, half:])
+    for i in range(terms_out.shape[0]):
+        term = mine * inner[i * rows : (i + 1) * rows]
+        terms_out[i : i + 1] = jnp.sum(term, axis=0, keepdims=True)
+
+
+def runs_kernel(mine, own, parts, tensor, runs, times, time_gram, both, bins_out):
+    half, width = own.shape
     rowcap = runs.shape[0]
     rows = times.shape[0]
-    bins = parts[...].reshape(rank, width)
-    bins_out[...] = bins
-    inner = quick(tensor[...], bins.astype(BF16), LAST)
+    core = lax.axis_index(PAIR)
+    rest = parts[...].reshape(half, width)
+    bins_out[pl.ds(core * half, half)] = own[...]
+    bins_out[pl.ds((1 - core) * half, half)] = rest
+    bins = bins_out[...]
+    inner = quick(tensor[...], rest.astype(BF16), LAST)
     mixing = exact(bins, bins, LAST) * time_gram[...]
     below = jnp.dot(runs[...], mixing, precision=HIGH)
+    full = times[...]
+    side = jnp.where(core == 0, full[:, half:], full[:, :half])
+    found = [
+        jnp.sum(side * inner[i * rows : (i + 1) * rows], axis=0, keepdims=True)
+        for i in range(rowcap)
+    ]
+    found = jnp.concatenate(found, axis=0)
+    first = jnp.where(core == 0, mine[...], found)
+    second = jnp.where(core == 0, found, mine[...])
+    terms = jnp.concatenate([first, second], axis=1)
     for copy in range(both.shape[0]):
         both[copy, rowcap:] = below
-    for i in range(rowcap):
-        term = jnp.sum(times[...] * inner[i * rows : (i + 1) * rows], axis=0, keepdims=True)
-        for copy in range(both.shape[0]):
-            both[copy, i : i + 1] = term
+        both[copy, 0:rowcap] = terms
 
 
 def last_kernel(count, parts, runs, out):
@@ -161,8 +197,9 @@
     rank = run_init.shape[1]
     flat = tensor.reshape(rowcap * rows, width)
     plane = extent(PLANE)
-    chunk = rank // plane
-    index = lax.axis_index(PLANE).reshape(1)
+    chunk = rank // (plane * extent(PAIR))
+    half = rank // extent(PAIR)
+    index = (lax.axis_index(PAIR) * half + lax.axis_index(PLANE) * chunk).reshape(1)
 
     both, runs, run_gram, pick, flat, bins, _, times = local(
         terms_kernel,
@@ -183,20 +220,26 @@
     )
     both = jnp.sum(exchange(both, NEAR), axis=0)
     both = exchange(jnp.broadcast_to(both[None], (extent(FAR),) + both.shape), FAR)
-    both, times, time_gram = local(
+    own, other, times, time_gram = local(
         time_kernel,
         (),
         (both, times, runs, run_gram, flat),
-        ((plane, chunk, width + rank), (rows, rank), (rank, rank)),
-    )
+        ((half, width + rank), (half, width + rank), (rows, rank), (rank, rank)),
+        scratch_shapes=[pltpu.VMEM((rank, width + rank), F32)],
+    )
+    other = swap(other)
+    (both,) = local(pair_kernel, (), (own, other), ((plane, chunk, width + rank),))
     both = exchange(both, PLANE)
     (both,) = local(spread_kernel, (), (both,), ((extent(FAR), chunk, width + rank),))
     both = exchange(both, FAR)
     (mine,) = local(bins_kernel, (), (both, bins, pick), ((plane, chunk, width),))
+    mine = exchange(mine, PLANE)
+    rest = swap(mine)
+    own, terms = local(half_kernel, (), (mine, flat, times), ((half, width), (rowcap, half)))
     both, bins = local(
         runs_kernel,
         (),
-        (exchange(mine, PLANE), flat, runs, times, time_gram),
+        (terms, own, rest, flat, runs, times, time_gram),
         ((extent(TM), 2 * rowcap, rank), (rank, width)),
     )
     both = exchange(both, TM)

time: 111 us -> 110 us (level)
  blocking collectives: 94 us -> 79 us
  starting transfers between devices: 3.75 us -> 15.1 us
  waiting for transfers between devices: 3.67 us -> 5.7 us
    all_to_all x5, blocking collectives: 94 us -> 79 us  [exchange(): return lax.all_to_all(parts, axes, 0, 0)]
    ppermute x0 -> x2, starting transfers between devices: none -> 11.4 us  [swap(): return lax.ppermute(value, PAIR, [(0, 1), (1, 0)])]
    ppermute x0 -> x2, waiting for transfers between devices: none -> 2.02 us  [swap(): return lax.ppermute(value, PAIR, [(0, 1), (1, 0)])]
    pallas_call x6 -> x8, Pallas kernels: 6.16 us -> 6.54 us  [local(): pl.pallas_call(kernel, out_shape=tuple((shape if hasattr(shape, 'dtype')...]
  transfers between devices with their start and end apart: 1 -> 3, of which waited for: 1 -> 3; matrix products, arithmetic and copies ran while one was open for 1% -> 1% of each run, Pallas kernels for 0% -> 0%
where the time goes in v5:
time: 110 us; the launch traced here: 109 us
  blocking collectives  79 us (72%)
  starting transfers between devices  15.1 us (14%)
  Pallas kernels  6.54 us (6%)
  waiting for transfers between devices  5.7 us (5%)
  local copies, waits for them, and re-layouts  1.6 us (1%)
  between operations  1.35 us (1%)
    all_to_all x5, blocking collectives, exchange(): return lax.all_to_all(parts, axes, 0, 0)  79 us
    ppermute x2, starting transfers between devices, swap(): return lax.ppermute(value, PAIR, [(0, 1), (1, 0)])  11.4 us
    pallas_call x8, Pallas kernels, local(): pl.pallas_call(kernel, out_shape=tuple((shape if hasattr(shape, 'dtype')...  6.54 us
    all_to_all x1, waiting for transfers between devices, exchange(): return lax.all_to_all(parts, axes, 0, 0)  3.67 us
    all_to_all x1, starting transfers between devices, exchange(): return lax.all_to_all(parts, axes, 0, 0)  3.64 us
  transfers between devices with their start and end apart: 3, of which 3 were waited for; matrix products, arithmetic and copies ran while one was open for 1% of the time, Pallas kernels for 0%

profile of v5, /device:TPU:1, one launch (start us, length us, event | category | flops | bytes accessed | tf_op | source)
XLA Modules:
  0.0 109.3 jit_solution(1019057091845962961)
XLA Ops:
  1.3 2.8 %shard_map.76 = (f32[8,32,128]{2,1,0:T(8,128)S(1)}, f32[16,128]{1,0:T(8,128)S(1)}, f32[128,128]{1,0:T(8,128)S(1)}, f32[2,128]{1,0:T(2,128)S(1)}, bf16[256,1024]{...) custom-call(s32[1]{0:T(128)S(6)} %copy.10.count, s32[1]{0:T(128)} %bitcast.index, ...), custom_call_target="tpu_custom_call" | custom-call | tf_op jit(solution)/shard_map/pallas_call | solution.py:183
  4.1 11.5 %all_to_all.30 = f32[8,32,128]{2,1,0:T(8,128)S(1)} all-to-all(f32[8,32,128]{2,1,0:T(8,128)S(1)} %get-tuple-element.18), channel_id=1, replica_groups=mesh['x'=4,'h'=8,'l'=2,'y'=4,'c'=2] {'x','l'}, dimensions={0} | all-to-all | bytes 262144 | tf_op jit(solution)/shard_map/all_to_all | solution.py:38
  15.7 27.0 %all_to_all.31.parts = f32[8,32,128]{2,1,0:T(8,128)S(1)} all-to-all(f32[8,32,128]{2,1,0:T(8,128)S(1)} %broadcast_in_dim.2), channel_id=1, replica_groups=mesh['x'=4,'h'=8,'l'=2,'y'=4,'c'=2] {'h'}, dimensions={0} | all-to-all | bytes 262144 | tf_op jit(solution)/shard_map/all_to_all | solution.py:38
  42.6 0.6 shard_map.77
  43.2 4.9 %collective-permute-start = (f32[64,1152]{1,0:T(8,128)S(1)}, f32[64,1152]{1,0:T(8,128)S(1)}, u32[]{:S(2)}, u32[]{:S(2)}) collective-permute-start(f32[64,1152]{1,0:T(8,128)S(1)} %get-tuple-element.24), channel_id=1, source_target_pairs={{0,1},{1,0},{2,3},{3,2},{4,5},{5,4},{6,7},{7,6},{8,9},{9,8},{10,11... | collective-permute-start | bytes 884744 | tf_op jit(solution)/shard_map/ppermute | solution.py:42
  48.1 1.2 %collective-permute-done.other = f32[64,1152]{1,0:T(8,128)S(1)} collective-permute-done((f32[64,1152]{1,0:T(8,128)S(1)}, f32[64,1152]{1,0:T(8,128)S(1)}, u32[]{:S(2)}, u32[]{:S(2)}) %collective-permute-start) | collective-permute-done | bytes 294944 | tf_op jit(solution)/shard_map/ppermute | solution.py:42
  49.3 0.1 shard_map.78
  49.3 13.7 %all_to_all.32.parts = f32[32,2,1152]{2,1,0:T(2,128)S(1)} all-to-all(f32[32,2,1152]{2,1,0:T(2,128)S(1)} %shard_map.78), channel_id=1, replica_groups=mesh['x'=4,'h'=8,'l'=2,'y'=4,'c'=2] {'x','l','y'}, dimensions={0} | all-to-all | bytes 589824 | tf_op jit(solution)/shard_map/all_to_all | solution.py:38
  63.0 14.9 %all_to_all.33.parts = f32[8,2,1152]{2,1,0:T(2,128)S(1)} all-to-all(f32[8,2,1152]{2,1,0:T(2,128)S(1)} %shard_map.79), channel_id=1, replica_groups=mesh['x'=4,'h'=8,'l'=2,'y'=4,'c'=2] {'h'}, dimensions={0} | all-to-all | bytes 147456 | tf_op jit(solution)/shard_map/all_to_all | solution.py:38
  77.9 0.5 shard_map.80
  78.5 11.9 %all_to_all.34.parts = f32[32,2,1024]{2,1,0:T(2,128)S(1)} all-to-all(f32[32,2,1024]{2,1,0:T(2,128)S(1)} %shard_map.80), channel_id=1, replica_groups=mesh['x'=4,'h'=8,'l'=2,'y'=4,'c'=2] {'x','l','y'}, dimensions={0} | all-to-all | bytes 524288 | tf_op jit(solution)/shard_map/all_to_all | solution.py:38
  90.4 6.6 %collective-permute-start.1 = (f32[32,2,1024]{2,1,0:T(2,128)S(1)}, f32[32,2,1024]{2,1,0:T(2,128)S(1)}, u32[]{:S(2)}, u32[]{:S(2)}) collective-permute-start(f32[32,2,1024]{2,1,0:T(2,128)S(1)} %all_to_all.34.parts), channel_id=1, source_target_pairs={{0,1},{1,0},{2,3},{3,2},{4,5},{5,4},{6,7},{7,6},{8,9},{9,8},{10,11... | collective-permute-start | bytes 786440 | tf_op jit(solution)/shard_map/ppermute | solution.py:42
  97.0 0.3 shard_map.81
  97.3 0.8 collective-permute-done.1.parts
  98.1 1.6 %shard_map.82 = (f32[8,32,128]{2,1,0:T(8,128)}, f32[128,1024]{1,0:T(8,128)S(1)}) custom-call(f32[16,64]{1,0:T(8,128)S(1)} %get-tuple-element.28.mine, f32[64,1024]{1,0:T(8,128)S(1)} %get-tuple-element.29.own, f32[32,2,1024]{2,1,0:T(2,128)S(1)} %collective-permute-done.1.parts, bf16[256,1024]{1,0:T(8,128)(2,1)S(1)} %get-tuple-element.22.tensor, ...), custom_call_target="tpu_custom_call" | custom-call | tf_op jit(solution)/shard_map/pallas_call | solution.py:183
  99.8 3.6 %all-to-all-start.5 = ((f32[8,32,128]{2,1,0:T(8,128)}), f32[8,32,128]{2,1,0:T(8,128)S(1)}, u32[]{:S(2)}, u32[]{:S(2)}) async-start(f32[8,32,128]{2,1,0:T(8,128)} %get-tuple-element.31), calls=%async_computation.5 | async-start | bytes 262144 | tf_op jit(solution)/shard_map/all_to_all | solution.py:38
  103.4 0.6 copy.9
  104.0 1.0 copy.8
  105.0 3.7 %all-to-all-done.5.parts = f32[8,32,128]{2,1,0:T(8,128)S(1)} async-done(((f32[8,32,128]{2,1,0:T(8,128)}), f32[8,32,128]{2,1,0:T(8,128)S(1)}, u32[]{:S(2)}, u32[]{:S(2)}) %all-to-all-start.5) | async-done | bytes 131104 | tf_op jit(solution)/shard_map/all_to_all | solution.py:38
  108.7 0.6 shard_map.83
  (3 shorter events, 0.1 us)
Async XLA Ops:
  43.2 6.1 %collective-permute-start = (f32[64,1152]{1,0:T(8,128)S(1)}, f32[64,1152]{1,0:T(8,128)S(1)}, u32[]{:S(2)}, u32[]{:S(2)}) collective-permute-start(f32[64,1152]{1,0:T(8,128)S(1)} %get-tuple-element.24), channel_id=1, source_target_pairs={{0,1},{1,0},{2,3},{3,2},{4,5},{5,4},{6,7},{7,6},{8,9},{9,8},{10,11... | collective-permute-start | bytes 884744 | tf_op jit(solution)/shard_map/ppermute | solution.py:42
  90.4 7.7 %collective-permute-start.1 = (f32[32,2,1024]{2,1,0:T(2,128)S(1)}, f32[32,2,1024]{2,1,0:T(2,128)S(1)}, u32[]{:S(2)}, u32[]{:S(2)}) collective-permute-start(f32[32,2,1024]{2,1,0:T(2,128)S(1)} %all_to_all.34.parts), channel_id=1, source_target_pairs={{0,1},{1,0},{2,3},{3,2},{4,5},{5,4},{6,7},{7,6},{8,9},{9,8},{10,11... | collective-permute-start | bytes 786440 | tf_op jit(solution)/shard_map/ppermute | solution.py:42
  99.8 8.9 %all-to-all-start.5 = ((f32[8,32,128]{2,1,0:T(8,128)}), f32[8,32,128]{2,1,0:T(8,128)S(1)}, u32[]{:S(2)}, u32[]{:S(2)}) async-start(f32[8,32,128]{2,1,0:T(8,128)} %get-tuple-element.31), calls=%async_computation.5 | async-start | bytes 262144 | tf_op jit(solution)/shard_map/all_to_all | solution.py:38

commit v6 on v5

v6 whole, which is shorter than its diff:
```python
import jax
import jax.numpy as jnp
from jax import lax
from jax.experimental import pallas as pl
from jax.experimental.pallas import tpu as pltpu
from jax.sharding import Mesh, PartitionSpec as P

HIGH = lax.Precision.HIGHEST
F32 = jnp.float32
BF16 = jnp.bfloat16
SIZES = {"x": 4, "h": 8, "l": 2, "y": 4, "c": 2}
RUNS = ("x", "h", "l")
NEAR = ("x", "l")
FAR = ("h",)
PLANE = ("x", "l", "y")
PAIR = ("c",)
TM = ("y", "c")
FIRST = (((0,), (0,)), ((), ()))
LAST = (((1,), (1,)), ((), ()))


def exact(left, right, dims):
    return lax.dot_general(left, right, dims, precision=HIGH, preferred_element_type=F32)


def quick(left, right, dims):
    return lax.dot_general(left, right, dims, preferred_element_type=F32)


def extent(axes):
    total = 1
    for axis in axes:
        total *= SIZES[axis]
    return total


def exchange(parts, axes):
    return lax.all_to_all(parts, axes, 0, 0)


def swap(value):
    return lax.ppermute(value, PAIR, [(0, 1), (1, 0)])


def added(parts):
    total = parts[0]
    for part in range(1, parts.shape[0]):
        total += parts[part]
    return total


def terms_kernel(*refs):
    far, (both, runs_out, gram_out, empty, *near), (sems,) = refs[:5], refs[5:13], refs[13:]
    tensor, bins, run_init, times = near
    copies = [pltpu.make_async_copy(far[i], near[i], sems.at[i]) for i in range(4)]
    for copy in reversed(copies):
        copy.start()
    rowcap, rank = run_init.shape
    rows = times.shape[0]
    slot = lax.broadcasted_iota(jnp.int32, (rowcap, rank), 0)
    for copy in reversed(copies[2:]):
        copy.wait()
    live = slot < far[4][0]
    empty[...] = jnp.where(live, 0.0, 1.0)
    runs = jnp.where(live, run_init[...], 0.0)
    runs_out[...] = runs
    run_gram = exact(runs, runs, FIRST)
    gram_out[...] = run_gram
    copies[1].wait()
    full = bins[...]
    below = jnp.dot(times[...], run_gram * exact(full, full, FIRST), precision=HIGH)
    copies[0].wait()
    inner = jnp.dot(tensor[...], full.astype(BF16), preferred_element_type=F32)
    terms = runs[0:1] * inner[0:rows]
    for i in range(1, rowcap):
        terms += runs[i : i + 1] * inner[i * rows : (i + 1) * rows]
    for copy in range(both.shape[0]):
        both[copy, 0:rows] = terms
        both[copy, rows:] = below


def pieces(value):
    out = []
    for _ in range(3):
        out.append(value.astype(BF16))
        value = value - out[-1].astype(F32)
    return out


def half_terms(runs, times, tensor, side):
    half = runs.shape[1] // 2
    runs, times = runs[...], times[...]
    low = times.astype(BF16).astype(F32)
    runs = jnp.where(side == 0, runs[:, :half], runs[:, half:])
    low = jnp.where(side == 0, low[:, :half], low[:, half:])
    left = jnp.concatenate([runs[i : i + 1] * low for i in range(runs.shape[0])], axis=0)
    block = tensor[...]
    high, mid, rest = (quick(part, block, FIRST) for part in pieces(left))
    return high + mid + rest


def time_kernel(parts, times, runs, run_gram, tensor, other, mixed, times_out, gram_out, whole):
    rows = times.shape[0]
    width = tensor.shape[1]
    half = other.shape[0]
    core = lax.axis_index(PAIR)
    sums = added(parts)
    new = times[...] * sums[:rows] / sums[rows:]
    times_out[...] = new
    time_gram = exact(new, new, FIRST)
    gram_out[...] = time_gram
    whole[...] = run_gram[...] * time_gram
    mixed[...] = whole[pl.ds(core * half, half)]
    other[:, 0:width] = half_terms(runs, times_out, tensor, 1 - core)
    other[:, width:] = whole[pl.ds((1 - core) * half, half)]


def side_kernel(runs, times, tensor, bins, own, *parts):
    own[...] = half_terms(runs, times, tensor, lax.axis_index(PAIR))
    for ref, part in zip(parts, pieces(bins[...].T)):
        ref[...] = part


def pair_kernel(own, mixed, other, out):
    count, chunk, width = out.shape
    inner = own.shape[1]
    got = other[...]
    out[:, :, 0:inner] = (own[...] + got[:, :inner]).reshape(count, chunk, inner)
    out[:, :, inner:] = (mixed[...] + got[:, inner:]).reshape(count, chunk, width - inner)


def spread_kernel(parts, out):
    total = added(parts)
    for copy in range(out.shape[0]):
        out[copy] = total


def bins_kernel(parts, high, mid, low, out):
    count, chunk, width = out.shape
    rank = high.shape[0]
    start = lax.axis_index(PAIR) * (count * chunk) + lax.axis_index(PLANE) * chunk
    sums = added(parts)
    row = lax.broadcasted_iota(jnp.int32, (chunk, rank), 0) + start
    column = lax.broadcasted_iota(jnp.int32, (chunk, rank), 1)
    pick = jnp.where(column == row, 1.0, 0.0)
    split = [part.astype(F32) for part in pieces(sums[:, width:])]
    left = jnp.concatenate([*split, pick], axis=0).astype(BF16)
    first, second, third = (jnp.dot(left, ref[...], preferred_element_type=F32) for ref in (high, mid, low))
    a, b, c, d = (slice(i * chunk, (i + 1) * chunk) for i in range(4))
    below = first[a] + (first[b] + second[a]) + (first[c] + second[b] + third[a])
    mine = (first[d] + second[d] + third[d]) * sums[:, :width] / below
    for copy in range(count):
        out[copy] = mine


def half_kernel(parts, tensor, times, bins_out, terms_out):
    half, width = bins_out.shape
    rows = times.shape[0]
    core = lax.axis_index(PAIR)
    bins = parts[...].reshape(half, width)
    bins_out[...] = bins
    inner = quick(tensor[...], bins.astype(BF16), LAST)
    both = times[...]
    mine = jnp.where(core == 0, both[:, :half], both[:, half:])
    for i in range(terms_out.shape[0]):
        term = mine * inner[i * rows : (i + 1) * rows]
        terms_out[i : i + 1] = jnp.sum(term, axis=0, keepdims=True)


def runs_kernel(mine, own, parts, tensor, runs, times, time_gram, both, bins_out):
    half, width = own.shape
    rowcap = runs.shape[0]
    rows = times.shape[0]
    core = lax.axis_index(PAIR)
    rest = parts[...].reshape(half, width)
    bins_out[pl.ds(core * half, half)] = own[...]
    bins_out[pl.ds((1 - core) * half, half)] = rest
    bins = bins_out[...]
    inner = quick(tensor[...], rest.astype(BF16), LAST)
    mixing = exact(bins, bins, LAST) * time_gram[...]
    below = jnp.dot(runs[...], mixing, precision=HIGH)
    full = times[...]
    side = jnp.where(core == 0, full[:, half:], full[:, :half])
    found = [
        jnp.sum(side * inner[i * rows : (i + 1) * rows], axis=0, keepdims=True)
        for i in range(rowcap)
    ]
    found = jnp.concatenate(found, axis=0)
    first = jnp.where(core == 0, mine[...], found)
    second = jnp.where(core == 0, found, mine[...])
    terms = jnp.concatenate([first, second], axis=1)
    for copy in range(both.shape[0]):
        both[copy, rowcap:] = below
        both[copy, 0:rowcap] = terms


def last_kernel(parts, runs, empty, out):
    rowcap = runs.shape[0]
    sums = added(parts)
    out[...] = runs[...] * sums[:rowcap] / (sums[rowcap:] + empty[...])


def shape_of(shape, dtype=F32):
    return pltpu.VMEM(shape, dtype)


def local(kernel, arrays, shapes, specs=None, **more):
    near = pl.BlockSpec(memory_space=pltpu.VMEM)
    if specs is None:
        arrays = [pltpu.with_memory_space_constraint(array, pltpu.VMEM) for array in arrays]
    return pl.pallas_call(
        kernel,
        out_shape=tuple(shapes),
        in_specs=specs or [near] * len(arrays),
        out_specs=(near,) * len(shapes),
        **more,
    )(*arrays)


def shards(tensor, run_counts, run_init, bin_init, time_init):
    rowcap, rows, width = tensor.shape
    rank = run_init.shape[1]
    flat = tensor.reshape(rowcap * rows, width)
    plane = extent(PLANE)
    half = rank // extent(PAIR)
    chunk = half // plane
    wide = width + rank

    both, runs, run_gram, empty, flat, bins, _, times = local(
        terms_kernel,
        (flat, bin_init, run_init, time_init, run_counts),
        (
            shape_of((extent(NEAR), 2 * rows, rank)),
            shape_of((rowcap, rank)),
            shape_of((rank, rank)),
            shape_of((rowcap, rank)),
            shape_of(flat.shape, flat.dtype),
            shape_of(bin_init.shape),
            shape_of((rowcap, rank)),
            shape_of((rows, rank)),
        ),
        [pl.BlockSpec(memory_space=pl.ANY)] * 4 + [pl.BlockSpec(memory_space=pltpu.SMEM)],
        scratch_shapes=[pltpu.SemaphoreType.DMA((4,))],
    )
    both = jnp.sum(exchange(both, NEAR), axis=0)
    both = exchange(jnp.broadcast_to(both[None], (extent(FAR),) + both.shape), FAR)
    other, mixed, times, time_gram = local(
        time_kernel,
        (both, times, runs, run_gram, flat),
        (shape_of((half, wide)), shape_of((half, rank)), shape_of((rows, rank)), shape_of((rank, rank))),
        scratch_shapes=[pltpu.VMEM((rank, rank), F32)],
    )
    other = swap(other)
    own, *parts = local(
        side_kernel,
        (runs, times, flat, bins),
        [shape_of((half, width))] + [shape_of((rank, width), BF16)] * 3,
    )
    (both,) = local(pair_kernel, (own, mixed, other), [shape_of((plane, chunk, wide))])
    both = exchange(both, PLANE)
    (both,) = local(spread_kernel, (both,), [shape_of((extent(FAR), chunk, wide))])
    both = exchange(both, FAR)
    (mine,) = local(bins_kernel, (both, *parts), [shape_of((plane, chunk, width))])
    mine = exchange(mine, PLANE)
    rest = swap(mine)
    own, terms = local(
        half_kernel, (mine, flat, times), (shape_of((half, width)), shape_of((rowcap, half)))
    )
    both, bins = local(
        runs_kernel,
        (terms, own, rest, flat, runs, times, time_gram),
        (shape_of((extent(TM), 2 * rowcap, rank)), shape_of((rank, width))),
    )
    both = exchange(both, TM)
    result = jax.ShapeDtypeStruct((rowcap, rank), F32)
    (runs,) = local(last_kernel, (both, runs, empty), [result])
    return (runs, bins.T, times)


def solution(mesh):
    fine = Mesh(mesh.devices.reshape(tuple(SIZES.values())), tuple(SIZES))
    return jax.shard_map(
        shards,
        mesh=fine,
        in_specs=(P(RUNS, TM, None), P(RUNS), P(RUNS, None), P(), P(TM, None)),
        out_specs=(P(RUNS, None), P(), P(TM, None)),
        check_vma=False,
    )
```

time: 110 us -> 109 us (level)
    pallas_call x8 -> x9, Pallas kernels: 6.54 us -> 6.67 us  [local(): pl.pallas_call(kernel, out_shape=tuple(shapes), in_specs=specs or [near]...]
  transfers between devices with their start and end apart: 3 -> 3, of which waited for: 3 -> 3; matrix products, arithmetic and copies ran while one was open for 1% -> 1% of each run, Pallas kernels for 0% -> 1%
where the time goes in v6:
time: 109 us
  blocking collectives  79 us (72%)
  starting transfers between devices  15.1 us (14%)
  Pallas kernels  6.67 us (6%)
  waiting for transfers between devices  5.21 us (5%)
  local copies, waits for them, and re-layouts  1.6 us (1%)
  between operations  1.34 us (1%)
    all_to_all x5, blocking collectives, exchange(): return lax.all_to_all(parts, axes, 0, 0)  79 us
    ppermute x2, starting transfers between devices, swap(): return lax.ppermute(value, PAIR, [(0, 1), (1, 0)])  11.4 us
    pallas_call x9, Pallas kernels, local(): pl.pallas_call(kernel, out_shape=tuple(shapes), in_specs=specs or [near]...  6.67 us
    all_to_all x1, waiting for transfers between devices, exchange(): return lax.all_to_all(parts, axes, 0, 0)  3.67 us
    all_to_all x1, starting transfers between devices, exchange(): return lax.all_to_all(parts, axes, 0, 0)  3.64 us
  transfers between devices with their start and end apart: 3, of which 3 were waited for; matrix products, arithmetic and copies ran while one was open for 1% of the time, Pallas kernels for 1%

profile of v6, /device:TPU:1, one launch (start us, length us, event | category | flops | bytes accessed | tf_op | source)
XLA Modules:
  0.0 108.9 jit_solution(17452400063598951827)
XLA Ops:
  1.3 2.8 %shard_map.76 = (f32[8,32,128]{2,1,0:T(8,128)S(1)}, f32[16,128]{1,0:T(8,128)S(1)}, f32[128,128]{1,0:T(8,128)S(1)}, f32[16,128]{1,0:T(8,128)S(1)}, bf16[256,1024]...) custom-call(bf16[256,1024]{1,0:T(8,128)(2,1)} %bitcast.3, ...), custom_call_target="tpu_custom_call" | custom-call | tf_op jit(solution)/shard_map/pallas_call | solution.py:211
  4.1 11.5 %all_to_all.30 = f32[8,32,128]{2,1,0:T(8,128)S(1)} all-to-all(f32[8,32,128]{2,1,0:T(8,128)S(1)} %get-tuple-element.23), channel_id=1, replica_groups=mesh['x'=4,'h'=8,'l'=2,'y'=4,'c'=2] {'x','l'}, dimensions={0} | all-to-all | bytes 262144 | tf_op jit(solution)/shard_map/all_to_all | solution.py:38
  15.6 27.0 %all_to_all.31.parts = f32[8,32,128]{2,1,0:T(8,128)S(1)} all-to-all(f32[8,32,128]{2,1,0:T(8,128)S(1)} %broadcast_in_dim.2), channel_id=1, replica_groups=mesh['x'=4,'h'=8,'l'=2,'y'=4,'c'=2] {'h'}, dimensions={0} | all-to-all | bytes 262144 | tf_op jit(solution)/shard_map/all_to_all | solution.py:38
  42.6 0.5 shard_map.77
  43.1 4.9 %collective-permute-start = (f32[64,1152]{1,0:T(8,128)S(1)}, f32[64,1152]{1,0:T(8,128)S(1)}, u32[]{:S(2)}, u32[]{:S(2)}) collective-permute-start(f32[64,1152]{1,0:T(8,128)S(1)} %get-tuple-element.31), channel_id=1, source_target_pairs={{0,1},{1,0},{2,3},{3,2},{4,5},{5,4},{6,7},{7,6},{8,9},{9,8},{10,11... | collective-permute-start | bytes 884744 | tf_op jit(solution)/shard_map/ppermute | solution.py:42
  48.0 0.5 shard_map.78
  48.5 0.7 collective-permute-done.other
  49.2 13.7 %all_to_all.32.parts = f32[32,2,1152]{2,1,0:T(2,128)S(1)} all-to-all(f32[32,2,1152]{2,1,0:T(2,128)S(1)} %shard_map.79), channel_id=1, replica_groups=mesh['x'=4,'h'=8,'l'=2,'y'=4,'c'=2] {'x','l','y'}, dimensions={0} | all-to-all | bytes 589824 | tf_op jit(solution)/shard_map/all_to_all | solution.py:38
  63.0 14.9 %all_to_all.33.parts = f32[8,2,1152]{2,1,0:T(2,128)S(1)} all-to-all(f32[8,2,1152]{2,1,0:T(2,128)S(1)} %shard_map.80), channel_id=1, replica_groups=mesh['x'=4,'h'=8,'l'=2,'y'=4,'c'=2] {'h'}, dimensions={0} | all-to-all | bytes 147456 | tf_op jit(solution)/shard_map/all_to_all | solution.py:38
  77.9 0.2 shard_map.81
  78.1 11.9 %all_to_all.34.parts = f32[32,2,1024]{2,1,0:T(2,128)S(1)} all-to-all(f32[32,2,1024]{2,1,0:T(2,128)S(1)} %shard_map.81), channel_id=1, replica_groups=mesh['x'=4,'h'=8,'l'=2,'y'=4,'c'=2] {'x','l','y'}, dimensions={0} | all-to-all | bytes 524288 | tf_op jit(solution)/shard_map/all_to_all | solution.py:38
  90.0 6.6 %collective-permute-start.1 = (f32[32,2,1024]{2,1,0:T(2,128)S(1)}, f32[32,2,1024]{2,1,0:T(2,128)S(1)}, u32[]{:S(2)}, u32[]{:S(2)}) collective-permute-start(f32[32,2,1024]{2,1,0:T(2,128)S(1)} %all_to_all.34.parts), channel_id=1, source_target_pairs={{0,1},{1,0},{2,3},{3,2},{4,5},{5,4},{6,7},{7,6},{8,9},{9,8},{10,11... | collective-permute-start | bytes 786440 | tf_op jit(solution)/shard_map/ppermute | solution.py:42
  96.6 0.3 shard_map.82
  96.9 0.8 collective-permute-done.1.parts
  97.8 1.6 %shard_map.83 = (f32[8,32,128]{2,1,0:T(8,128)}, f32[128,1024]{1,0:T(8,128)S(1)}) custom-call(f32[16,64]{1,0:T(8,128)S(1)} %get-tuple-element.35.mine, f32[64,1024]{1,0:T(8,128)S(1)} %get-tuple-element.36.own, f32[32,2,1024]{2,1,0:T(2,128)S(1)} %collective-permute-done.1.parts, bf16[256,1024]{1,0:T(8,128)(2,1)S(1)} %get-tuple-element.26.tensor, ...), custom_call_target="tpu_custom_call" | custom-call | tf_op jit(solution)/shard_map/pallas_call | solution.py:211
  99.4 3.6 %all-to-all-start.5 = ((f32[8,32,128]{2,1,0:T(8,128)}), f32[8,32,128]{2,1,0:T(8,128)S(1)}, u32[]{:S(2)}, u32[]{:S(2)}) async-start(f32[8,32,128]{2,1,0:T(8,128)} %get-tuple-element.38), calls=%async_computation.5 | async-start | bytes 262144 | tf_op jit(solution)/shard_map/all_to_all | solution.py:38
  103.0 0.6 copy.9
  103.6 1.0 copy.8
  104.6 3.7 %all-to-all-done.5.parts = f32[8,32,128]{2,1,0:T(8,128)S(1)} async-done(((f32[8,32,128]{2,1,0:T(8,128)}), f32[8,32,128]{2,1,0:T(8,128)S(1)}, u32[]{:S(2)}, u32[]{:S(2)}) %all-to-all-start.5) | async-done | bytes 131104 | tf_op jit(solution)/shard_map/all_to_all | solution.py:38
  108.3 0.6 shard_map.84
  (4 shorter events, 0.1 us)
Async XLA Ops:
  43.1 6.1 %collective-permute-start = (f32[64,1152]{1,0:T(8,128)S(1)}, f32[64,1152]{1,0:T(8,128)S(1)}, u32[]{:S(2)}, u32[]{:S(2)}) collective-permute-start(f32[64,1152]{1,0:T(8,128)S(1)} %get-tuple-element.31), channel_id=1, source_target_pairs={{0,1},{1,0},{2,3},{3,2},{4,5},{5,4},{6,7},{7,6},{8,9},{9,8},{10,11... | collective-permute-start | bytes 884744 | tf_op jit(solution)/shard_map/ppermute | solution.py:42
  90.0 7.7 %collective-permute-start.1 = (f32[32,2,1024]{2,1,0:T(2,128)S(1)}, f32[32,2,1024]{2,1,0:T(2,128)S(1)}, u32[]{:S(2)}, u32[]{:S(2)}) collective-permute-start(f32[32,2,1024]{2,1,0:T(2,128)S(1)} %all_to_all.34.parts), channel_id=1, source_target_pairs={{0,1},{1,0},{2,3},{3,2},{4,5},{5,4},{6,7},{7,6},{8,9},{9,8},{10,11... | collective-permute-start | bytes 786440 | tf_op jit(solution)/shard_map/ppermute | solution.py:42
  99.4 8.9 %all-to-all-start.5 = ((f32[8,32,128]{2,1,0:T(8,128)}), f32[8,32,128]{2,1,0:T(8,128)S(1)}, u32[]{:S(2)}, u32[]{:S(2)}) async-start(f32[8,32,128]{2,1,0:T(8,128)} %get-tuple-element.38), calls=%async_computation.5 | async-start | bytes 262144 | tf_op jit(solution)/shard_map/all_to_all | solution.py:38

commit v7 on v6

--- a/solution.py
+++ b/solution.py
@@ -167,7 +167,7 @@
         terms_out[i : i + 1] = jnp.sum(term, axis=0, keepdims=True)
 
 
-def runs_kernel(mine, own, parts, tensor, runs, times, time_gram, both, bins_out):
+def runs_kernel(mine, own, parts, tensor, runs, times, time_gram, both, turned, bins_out):
     half, width = own.shape
     rowcap = runs.shape[0]
     rows = times.shape[0]
@@ -176,6 +176,7 @@
     bins_out[pl.ds(core * half, half)] = own[...]
     bins_out[pl.ds((1 - core) * half, half)] = rest
     bins = bins_out[...]
+    turned[...] = bins.T
     inner = quick(tensor[...], rest.astype(BF16), LAST)
     mixing = exact(bins, bins, LAST) * time_gram[...]
     below = jnp.dot(runs[...], mixing, precision=HIGH)
@@ -194,17 +195,26 @@
         both[copy, 0:rowcap] = terms
 
 
-def last_kernel(parts, runs, empty, out):
+def last_kernel(parts, runs, empty, bins, times, runs_out, bins_out, times_out, new, sems):
+    copies = [
+        pltpu.make_async_copy(near, far, sems.at[i])
+        for i, (near, far) in enumerate(((bins, bins_out), (times, times_out), (new, runs_out)))
+    ]
+    copies[0].start()
+    copies[1].start()
     rowcap = runs.shape[0]
     sums = added(parts)
-    out[...] = runs[...] * sums[:rowcap] / (sums[rowcap:] + empty[...])
+    new[...] = runs[...] * sums[:rowcap] / (sums[rowcap:] + empty[...])
+    copies[2].start()
+    for copy in copies:
+        copy.wait()
 
 
 def shape_of(shape, dtype=F32):
     return pltpu.VMEM(shape, dtype)
 
 
-def local(kernel, arrays, shapes, specs=None, **more):
+def local(kernel, arrays, shapes, specs=None, outs=pltpu.VMEM, **more):
     near = pl.BlockSpec(memory_space=pltpu.VMEM)
     if specs is None:
         arrays = [pltpu.with_memory_space_constraint(array, pltpu.VMEM) for array in arrays]
@@ -212,7 +222,7 @@
         kernel,
         out_shape=tuple(shapes),
         in_specs=specs or [near] * len(arrays),
-        out_specs=(near,) * len(shapes),
+        out_specs=(pl.BlockSpec(memory_space=outs),) * len(shapes),
         **more,
     )(*arrays)
 
@@ -269,12 +279,18 @@
     both, bins = local(
         runs_kernel,
         (terms, own, rest, flat, runs, times, time_gram),
-        (shape_of((extent(TM), 2 * rowcap, rank)), shape_of((rank, width))),
-    )
-    both = exchange(both, TM)
-    result = jax.ShapeDtypeStruct((rowcap, rank), F32)
-    (runs,) = local(last_kernel, (both, runs, empty), [result])
-    return (runs, bins.T, times)
+        (shape_of((extent(TM), 2 * rowcap, rank)), shape_of((width, rank))),
+        scratch_shapes=[pltpu.VMEM((rank, width), F32)],
+    )
+    return tuple(
+        local(
+            last_kernel,
+            (exchange(both, TM), runs, empty, bins, times),
+            [jax.ShapeDtypeStruct(shape, F32) for shape in (runs.shape, bins.shape, times.shape)],
+            outs=pl.ANY,
+            scratch_shapes=[pltpu.VMEM(runs.shape, F32), pltpu.SemaphoreType.DMA((3,))],
+        )
+    )
 
 
 def solution(mesh):

time: 109 us -> 108 us (level)
  blocking collectives: 79 us -> 87.2 us
  starting transfers between devices: 15.1 us -> 11.4 us
  waiting for transfers between devices: 5.21 us -> 1.53 us
  local copies, waits for them, and re-layouts: 1.6 us -> 0.01 us
    all_to_all x5 -> x6, blocking collectives: 79 us -> 87.2 us  [exchange(): return lax.all_to_all(parts, axes, 0, 0)]
    all_to_all x1 -> x0, waiting for transfers between devices: 3.67 us -> none  [exchange(): return lax.all_to_all(parts, axes, 0, 0)]
    all_to_all x1 -> x0, starting transfers between devices: 3.64 us -> none  [exchange(): return lax.all_to_all(parts, axes, 0, 0)]
    unnamed x2 -> x0, local copies, waits for them, and re-layouts: 1.59 us -> none
  transfers between devices with their start and end apart: 3 -> 2, of which waited for: 3 -> 2; matrix products, arithmetic and copies ran while one was open for 1% -> 0% of each run, Pallas kernels for 1% -> 1%
where the time goes in v7:
time: 108 us
  blocking collectives  87.2 us (81%)
  starting transfers between devices  11.4 us (11%)
  Pallas kernels  6.21 us (6%)
  waiting for transfers between devices  1.53 us (1%)
  between operations  1.34 us (1%)
    all_to_all x6, blocking collectives, exchange(): return lax.all_to_all(parts, axes, 0, 0)  87.2 us
    ppermute x2, starting transfers between devices, swap(): return lax.ppermute(value, PAIR, [(0, 1), (1, 0)])  11.4 us
    pallas_call x9, Pallas kernels, local(): pl.pallas_call(kernel, out_shape=tuple(shapes), in_specs=specs or [near]...  6.21 us
  transfers between devices with their start and end apart: 2, of which 2 were waited for; matrix products, arithmetic and copies ran while one was open for 0% of the time, Pallas kernels for 1%

profile of v7, /device:TPU:1, one launch (start us, length us, event | category | flops | bytes accessed | tf_op | source)
XLA Modules:
  0.0 107.8 jit_solution(4576526482914594660)
XLA Ops:
  1.3 2.8 %shard_map.76 = (f32[8,32,128]{2,1,0:T(8,128)S(1)}, f32[16,128]{1,0:T(8,128)S(1)}, f32[128,128]{1,0:T(8,128)S(1)}, f32[16,128]{1,0:T(8,128)S(1)}, bf16[256,1024]...) custom-call(bf16[256,1024]{1,0:T(8,128)(2,1)} %bitcast.1, ...), custom_call_target="tpu_custom_call" | custom-call | tf_op jit(solution)/shard_map/pallas_call | solution.py:221
  4.1 11.5 %all_to_all.30 = f32[8,32,128]{2,1,0:T(8,128)S(1)} all-to-all(f32[8,32,128]{2,1,0:T(8,128)S(1)} %get-tuple-element.23), channel_id=1, replica_groups=mesh['x'=4,'h'=8,'l'=2,'y'=4,'c'=2] {'x','l'}, dimensions={0} | all-to-all | bytes 262144 | tf_op jit(solution)/shard_map/all_to_all | solution.py:38
  15.6 27.0 %all_to_all.31.parts = f32[8,32,128]{2,1,0:T(8,128)S(1)} all-to-all(f32[8,32,128]{2,1,0:T(8,128)S(1)} %broadcast_in_dim.2), channel_id=1, replica_groups=mesh['x'=4,'h'=8,'l'=2,'y'=4,'c'=2] {'h'}, dimensions={0} | all-to-all | bytes 262144 | tf_op jit(solution)/shard_map/all_to_all | solution.py:38
  42.6 0.5 shard_map.77
  43.1 4.9 %collective-permute-start = (f32[64,1152]{1,0:T(8,128)S(1)}, f32[64,1152]{1,0:T(8,128)S(1)}, u32[]{:S(2)}, u32[]{:S(2)}) collective-permute-start(f32[64,1152]{1,0:T(8,128)S(1)} %get-tuple-element.31), channel_id=1, source_target_pairs={{0,1},{1,0},{2,3},{3,2},{4,5},{5,4},{6,7},{7,6},{8,9},{9,8},{10,11... | collective-permute-start | bytes 884744 | tf_op jit(solution)/shard_map/ppermute | solution.py:42
  48.0 0.5 shard_map.78
  48.5 0.7 collective-permute-done.other
  49.2 13.7 %all_to_all.32.parts = f32[32,2,1152]{2,1,0:T(2,128)S(1)} all-to-all(f32[32,2,1152]{2,1,0:T(2,128)S(1)} %shard_map.79), channel_id=1, replica_groups=mesh['x'=4,'h'=8,'l'=2,'y'=4,'c'=2] {'x','l','y'}, dimensions={0} | all-to-all | bytes 589824 | tf_op jit(solution)/shard_map/all_to_all | solution.py:38
  63.0 14.9 %all_to_all.33.parts = f32[8,2,1152]{2,1,0:T(2,128)S(1)} all-to-all(f32[8,2,1152]{2,1,0:T(2,128)S(1)} %shard_map.80), channel_id=1, replica_groups=mesh['x'=4,'h'=8,'l'=2,'y'=4,'c'=2] {'h'}, dimensions={0} | all-to-all | bytes 147456 | tf_op jit(solution)/shard_map/all_to_all | solution.py:38
  77.8 0.2 shard_map.81
  78.1 11.9 %all_to_all.34.parts = f32[32,2,1024]{2,1,0:T(2,128)S(1)} all-to-all(f32[32,2,1024]{2,1,0:T(2,128)S(1)} %shard_map.81), channel_id=1, replica_groups=mesh['x'=4,'h'=8,'l'=2,'y'=4,'c'=2] {'x','l','y'}, dimensions={0} | all-to-all | bytes 524288 | tf_op jit(solution)/shard_map/all_to_all | solution.py:38
  90.0 6.6 %collective-permute-start.1 = (f32[32,2,1024]{2,1,0:T(2,128)S(1)}, f32[32,2,1024]{2,1,0:T(2,128)S(1)}, u32[]{:S(2)}, u32[]{:S(2)}) collective-permute-start(f32[32,2,1024]{2,1,0:T(2,128)S(1)} %all_to_all.34.parts), channel_id=1, source_target_pairs={{0,1},{1,0},{2,3},{3,2},{4,5},{5,4},{6,7},{7,6},{8,9},{9,8},{10,11... | collective-permute-start | bytes 786440 | tf_op jit(solution)/shard_map/ppermute | solution.py:42
  96.6 0.3 shard_map.82
  96.9 0.8 collective-permute-done.1.parts
  97.7 1.0 shard_map.83
  98.7 8.2 %all_to_all.35.parts = f32[8,32,128]{2,1,0:T(8,128)S(1)} all-to-all(f32[8,32,128]{2,1,0:T(8,128)S(1)} %get-tuple-element.38), channel_id=1, replica_groups=mesh['x'=4,'h'=8,'l'=2,'y'=4,'c'=2] {'y','c'}, dimensions={0} | all-to-all | bytes 262144 | tf_op jit(solution)/shard_map/all_to_all | solution.py:38
  106.9 0.8 shard_map.84
  (4 shorter events, 0.1 us)
Async XLA Ops:
  43.1 6.1 %collective-permute-start = (f32[64,1152]{1,0:T(8,128)S(1)}, f32[64,1152]{1,0:T(8,128)S(1)}, u32[]{:S(2)}, u32[]{:S(2)}) collective-permute-start(f32[64,1152]{1,0:T(8,128)S(1)} %get-tuple-element.31), channel_id=1, source_target_pairs={{0,1},{1,0},{2,3},{3,2},{4,5},{5,4},{6,7},{7,6},{8,9},{9,8},{10,11... | collective-permute-start | bytes 884744 | tf_op jit(solution)/shard_map/ppermute | solution.py:42
  90.0 7.7 %collective-permute-start.1 = (f32[32,2,1024]{2,1,0:T(2,128)S(1)}, f32[32,2,1024]{2,1,0:T(2,128)S(1)}, u32[]{:S(2)}, u32[]{:S(2)}) collective-permute-start(f32[32,2,1024]{2,1,0:T(2,128)S(1)} %all_to_all.34.parts), channel_id=1, source_target_pairs={{0,1},{1,0},{2,3},{3,2},{4,5},{5,4},{6,7},{7,6},{8,9},{9,8},{10,11... | collective-permute-start | bytes 786440 | tf_op jit(solution)/shard_map/ppermute | solution.py:42

commit v8 on v7

--- a/solution.py
+++ b/solution.py
@@ -49,34 +49,38 @@
     return total
 
 
-def terms_kernel(*refs):
-    far, (both, runs_out, gram_out, empty, *near), (sems,) = refs[:5], refs[5:13], refs[13:]
-    tensor, bins, run_init, times = near
-    copies = [pltpu.make_async_copy(far[i], near[i], sems.at[i]) for i in range(4)]
+def grams_kernel(*refs):
+    far, count = refs[:3], refs[3]
+    runs_out, gram_out, empty, low, below, *near, sems = refs[4:]
+    bins, run_init, times = near
+    copies = [pltpu.make_async_copy(far[i], near[i], sems.at[i]) for i in range(3)]
     for copy in reversed(copies):
         copy.start()
-    rowcap, rank = run_init.shape
-    rows = times.shape[0]
-    slot = lax.broadcasted_iota(jnp.int32, (rowcap, rank), 0)
-    for copy in reversed(copies[2:]):
-        copy.wait()
-    live = slot < far[4][0]
+    slot = lax.broadcasted_iota(jnp.int32, run_init.shape, 0)
+    copies[1].wait()
+    live = slot < count[0]
     empty[...] = jnp.where(live, 0.0, 1.0)
     runs = jnp.where(live, run_init[...], 0.0)
     runs_out[...] = runs
     run_gram = exact(runs, runs, FIRST)
     gram_out[...] = run_gram
-    copies[1].wait()
+    copies[2].wait()
+    copies[0].wait()
     full = bins[...]
-    below = jnp.dot(times[...], run_gram * exact(full, full, FIRST), precision=HIGH)
-    copies[0].wait()
-    inner = jnp.dot(tensor[...], full.astype(BF16), preferred_element_type=F32)
+    low[...] = full.astype(BF16)
+    below[...] = jnp.dot(times[...], run_gram * square(full, FIRST), precision=HIGH)
+
+
+def terms_kernel(tensor, low, runs, below, both):
+    rowcap = runs.shape[0]
+    rows = below.shape[0]
+    inner = jnp.dot(tensor[...], low[...], preferred_element_type=F32)
     terms = runs[0:1] * inner[0:rows]
     for i in range(1, rowcap):
         terms += runs[i : i + 1] * inner[i * rows : (i + 1) * rows]
     for copy in range(both.shape[0]):
         both[copy, 0:rows] = terms
-        both[copy, rows:] = below
+        both[copy, rows:] = below[...]
 
 
 def pieces(value):
@@ -85,6 +89,13 @@
         out.append(value.astype(BF16))
         value = value - out[-1].astype(F32)
     return out
+
+
+def square(value, dims):
+    high, mid, low = pieces(value)
+    cross = quick(high, mid, dims)
+    far = quick(high, low, dims)
+    return quick(high, high, dims) + (cross + cross.T) + (quick(mid, mid, dims) + far + far.T)
 
 
 def half_terms(runs, times, tensor, side):
@@ -236,22 +247,25 @@
     chunk = half // plane
     wide = width + rank
 
-    both, runs, run_gram, empty, flat, bins, _, times = local(
-        terms_kernel,
-        (flat, bin_init, run_init, time_init, run_counts),
+    flat = pltpu.with_memory_space_constraint(flat, pltpu.VMEM)
+    runs, run_gram, empty, low, below, bins, _, times = local(
+        grams_kernel,
+        (bin_init, run_init, time_init, run_counts),
         (
-            shape_of((extent(NEAR), 2 * rows, rank)),
             shape_of((rowcap, rank)),
             shape_of((rank, rank)),
             shape_of((rowcap, rank)),
-            shape_of(flat.shape, flat.dtype),
+            shape_of(bin_init.shape, BF16),
+            shape_of((rows, rank)),
             shape_of(bin_init.shape),
             shape_of((rowcap, rank)),
             shape_of((rows, rank)),
         ),
-        [pl.BlockSpec(memory_space=pl.ANY)] * 4 + [pl.BlockSpec(memory_space=pltpu.SMEM)],
-        scratch_shapes=[pltpu.SemaphoreType.DMA((4,))],
-    )
+        [pl.BlockSpec(memory_space=space) for space in (*[pl.ANY] * 3, pltpu.SMEM)],
+        scratch_shapes=[pltpu.SemaphoreType.DMA((3,))],
+    )
+    shape = (extent(NEAR), 2 * rows, rank)
+    (both,) = local(terms_kernel, (flat, low, runs, below), [shape_of(shape)])
     both = jnp.sum(exchange(both, NEAR), axis=0)
     both = exchange(jnp.broadcast_to(both[None], (extent(FAR),) + both.shape), FAR)
     other, mixed, times, time_gram = local(

time: 108 us -> 108 us (level)
    pallas_call x9 -> x10, Pallas kernels: 6.21 us -> 5.9 us  [local(): pl.pallas_call(kernel, out_shape=tuple(shapes), in_specs=specs or [near]...]
where the time goes in v8:
time: 108 us
  blocking collectives  87.2 us (81%)
  starting transfers between devices  11.4 us (11%)
  Pallas kernels  5.9 us (5%)
  waiting for transfers between devices  1.53 us (1%)
  between operations  1.42 us (1%)
    all_to_all x6, blocking collectives, exchange(): return lax.all_to_all(parts, axes, 0, 0)  87.2 us
    ppermute x2, starting transfers between devices, swap(): return lax.ppermute(value, PAIR, [(0, 1), (1, 0)])  11.4 us
    pallas_call x10, Pallas kernels, local(): pl.pallas_call(kernel, out_shape=tuple(shapes), in_specs=specs or [near]...  5.9 us
  transfers between devices with their start and end apart: 2, of which 2 were waited for; matrix products, arithmetic and copies ran while one was open for 0% of the time, Pallas kernels for 1%

profile of v8, /device:TPU:1, one launch (start us, length us, event | category | flops | bytes accessed | tf_op | source)
XLA Modules:
  0.0 107.5 jit_solution(182757112786291367)
XLA Ops:
  0.6 0.0 copy-start
  1.3 2.2 %shard_map.76 = (f32[16,128]{1,0:T(8,128)S(1)}, f32[128,128]{1,0:T(8,128)S(1)}, f32[16,128]{1,0:T(8,128)S(1)}, bf16[1024,128]{1,0:T(8,128)(2,1)S(1)}, f32[16,128...) custom-call(f32[1024,128]{1,0:T(8,128)} %refs_0_.1, f32[16,128]{1,0:T(8,128)} %refs_1_.1, ...), custom_call_target="tpu_custom_call" | custom-call | tf_op jit(solution)/shard_map/pallas_call | solution.py:232
  3.5 0.0 copy-done
  3.5 0.3 shard_map.77
  3.8 11.5 %all_to_all.30 = f32[8,32,128]{2,1,0:T(8,128)S(1)} all-to-all(f32[8,32,128]{2,1,0:T(8,128)S(1)} %shard_map.77), channel_id=1, replica_groups=mesh['x'=4,'h'=8,'l'=2,'y'=4,'c'=2] {'x','l'}, dimensions={0} | all-to-all | bytes 262144 | tf_op jit(solution)/shard_map/all_to_all | solution.py:38
  15.4 27.0 %all_to_all.31.parts = f32[8,32,128]{2,1,0:T(8,128)S(1)} all-to-all(f32[8,32,128]{2,1,0:T(8,128)S(1)} %broadcast_in_dim.2), channel_id=1, replica_groups=mesh['x'=4,'h'=8,'l'=2,'y'=4,'c'=2] {'h'}, dimensions={0} | all-to-all | bytes 262144 | tf_op jit(solution)/shard_map/all_to_all | solution.py:38
  42.4 0.5 shard_map.78
  42.9 4.9 %collective-permute-start = (f32[64,1152]{1,0:T(8,128)S(1)}, f32[64,1152]{1,0:T(8,128)S(1)}, u32[]{:S(2)}, u32[]{:S(2)}) collective-permute-start(f32[64,1152]{1,0:T(8,128)S(1)} %get-tuple-element.31), channel_id=1, source_target_pairs={{0,1},{1,0},{2,3},{3,2},{4,5},{5,4},{6,7},{7,6},{8,9},{9,8},{10,11... | collective-permute-start | bytes 884744 | tf_op jit(solution)/shard_map/ppermute | solution.py:42
  47.8 0.5 shard_map.79
  48.3 0.7 collective-permute-done.other
  49.0 13.7 %all_to_all.32.parts = f32[32,2,1152]{2,1,0:T(2,128)S(1)} all-to-all(f32[32,2,1152]{2,1,0:T(2,128)S(1)} %shard_map.80), channel_id=1, replica_groups=mesh['x'=4,'h'=8,'l'=2,'y'=4,'c'=2] {'x','l','y'}, dimensions={0} | all-to-all | bytes 589824 | tf_op jit(solution)/shard_map/all_to_all | solution.py:38
  62.7 14.9 %all_to_all.33.parts = f32[8,2,1152]{2,1,0:T(2,128)S(1)} all-to-all(f32[8,2,1152]{2,1,0:T(2,128)S(1)} %shard_map.81), channel_id=1, replica_groups=mesh['x'=4,'h'=8,'l'=2,'y'=4,'c'=2] {'h'}, dimensions={0} | all-to-all | bytes 147456 | tf_op jit(solution)/shard_map/all_to_all | solution.py:38
  77.6 0.2 shard_map.82
  77.9 11.9 %all_to_all.34.parts = f32[32,2,1024]{2,1,0:T(2,128)S(1)} all-to-all(f32[32,2,1024]{2,1,0:T(2,128)S(1)} %shard_map.82), channel_id=1, replica_groups=mesh['x'=4,'h'=8,'l'=2,'y'=4,'c'=2] {'x','l','y'}, dimensions={0} | all-to-all | bytes 524288 | tf_op jit(solution)/shard_map/all_to_all | solution.py:38
  89.8 6.6 %collective-permute-start.1 = (f32[32,2,1024]{2,1,0:T(2,128)S(1)}, f32[32,2,1024]{2,1,0:T(2,128)S(1)}, u32[]{:S(2)}, u32[]{:S(2)}) collective-permute-start(f32[32,2,1024]{2,1,0:T(2,128)S(1)} %all_to_all.34.parts), channel_id=1, source_target_pairs={{0,1},{1,0},{2,3},{3,2},{4,5},{5,4},{6,7},{7,6},{8,9},{9,8},{10,11... | collective-permute-start | bytes 786440 | tf_op jit(solution)/shard_map/ppermute | solution.py:42
  96.4 0.3 shard_map.83
  96.7 0.8 collective-permute-done.1.parts
  97.5 1.0 shard_map.84
  98.5 8.2 %all_to_all.35.parts = f32[8,32,128]{2,1,0:T(8,128)S(1)} all-to-all(f32[8,32,128]{2,1,0:T(8,128)S(1)} %get-tuple-element.38), channel_id=1, replica_groups=mesh['x'=4,'h'=8,'l'=2,'y'=4,'c'=2] {'y','c'}, dimensions={0} | all-to-all | bytes 262144 | tf_op jit(solution)/shard_map/all_to_all | solution.py:38
  106.7 0.8 shard_map.85
  (4 shorter events, 0.1 us)
Async XLA Ops:
  0.6 2.9 %copy-start = (bf16[16,16,1024]{2,1,0:T(8,128)(2,1)S(1)}, bf16[16,16,1024]{2,1,0:T(8,128)(2,1)}, u32[]{:S(2)}) copy-start(bf16[16,16,1024]{2,1,0:T(8,128)(2,1)} %param.5) | copy-start | bytes 1572868
  42.9 6.1 %collective-permute-start = (f32[64,1152]{1,0:T(8,128)S(1)}, f32[64,1152]{1,0:T(8,128)S(1)}, u32[]{:S(2)}, u32[]{:S(2)}) collective-permute-start(f32[64,1152]{1,0:T(8,128)S(1)} %get-tuple-element.31), channel_id=1, source_target_pairs={{0,1},{1,0},{2,3},{3,2},{4,5},{5,4},{6,7},{7,6},{8,9},{9,8},{10,11... | collective-permute-start | bytes 884744 | tf_op jit(solution)/shard_map/ppermute | solution.py:42
  89.8 7.7 %collective-permute-start.1 = (f32[32,2,1024]{2,1,0:T(2,128)S(1)}, f32[32,2,1024]{2,1,0:T(2,128)S(1)}, u32[]{:S(2)}, u32[]{:S(2)}) collective-permute-start(f32[32,2,1024]{2,1,0:T(2,128)S(1)} %all_to_all.34.parts), channel_id=1, source_target_pairs={{0,1},{1,0},{2,3},{3,2},{4,5},{5,4},{6,7},{7,6},{8,9},{9,8},{10,11... | collective-permute-start | bytes 786440 | tf_op jit(solution)/shard_map/ppermute | solution.py:42

commit v9 on v7

--- a/solution.py
+++ b/solution.py
@@ -240,7 +240,7 @@
         terms_kernel,
         (flat, bin_init, run_init, time_init, run_counts),
         (
-            shape_of((extent(NEAR), 2 * rows, rank)),
+            shape_of((extent(FAR), 2 * rows, rank)),
             shape_of((rowcap, rank)),
             shape_of((rank, rank)),
             shape_of((rowcap, rank)),
@@ -252,8 +252,8 @@
         [pl.BlockSpec(memory_space=pl.ANY)] * 4 + [pl.BlockSpec(memory_space=pltpu.SMEM)],
         scratch_shapes=[pltpu.SemaphoreType.DMA((4,))],
     )
-    both = jnp.sum(exchange(both, NEAR), axis=0)
-    both = exchange(jnp.broadcast_to(both[None], (extent(FAR),) + both.shape), FAR)
+    both = jnp.sum(exchange(both, FAR), axis=0)
+    both = exchange(jnp.broadcast_to(both[None], (extent(NEAR),) + both.shape), NEAR)
     other, mixed, times, time_gram = local(
         time_kernel,
         (both, times, runs, run_gram, flat),

time: 108 us -> 109 us (level)
  starting transfers between devices: 11.4 us -> 12.6 us
    ppermute x2, starting transfers between devices: 11.4 us -> 12.6 us  [swap(): return lax.ppermute(value, PAIR, [(0, 1), (1, 0)])]
where the time goes in v9:
time: 109 us
  blocking collectives  87.2 us (80%)
  starting transfers between devices  12.6 us (12%)
  Pallas kernels  6.22 us (6%)
  waiting for transfers between devices  1.53 us (1%)
  between operations  1.34 us (1%)
    all_to_all x6, blocking collectives, exchange(): return lax.all_to_all(parts, axes, 0, 0)  87.2 us
    ppermute x2, starting transfers between devices, swap(): return lax.ppermute(value, PAIR, [(0, 1), (1, 0)])  12.6 us
    pallas_call x9, Pallas kernels, local(): pl.pallas_call(kernel, out_shape=tuple(shapes), in_specs=specs or [near]...  6.22 us
  transfers between devices with their start and end apart: 2, of which 2 were waited for; matrix products, arithmetic and copies ran while one was open for 0% of the time, Pallas kernels for 1%

profile of v9, /device:TPU:1, one launch (start us, length us, event | category | flops | bytes accessed | tf_op | source)
XLA Modules:
  0.0 109.0 jit_solution(15420905015269532051)
XLA Ops:
  1.3 2.8 %shard_map.76 = (f32[8,32,128]{2,1,0:T(8,128)S(1)}, f32[16,128]{1,0:T(8,128)S(1)}, f32[128,128]{1,0:T(8,128)S(1)}, f32[16,128]{1,0:T(8,128)S(1)}, bf16[256,1024]...) custom-call(bf16[256,1024]{1,0:T(8,128)(2,1)} %bitcast.1, ...), custom_call_target="tpu_custom_call" | custom-call | tf_op jit(solution)/shard_map/pallas_call | solution.py:221
  4.1 28.6 %all_to_all.30 = f32[8,32,128]{2,1,0:T(8,128)S(1)} all-to-all(f32[8,32,128]{2,1,0:T(8,128)S(1)} %get-tuple-element.23), channel_id=1, replica_groups=mesh['x'=4,'h'=8,'l'=2,'y'=4,'c'=2] {'h'}, dimensions={0} | all-to-all | bytes 262144 | tf_op jit(solution)/shard_map/all_to_all | solution.py:38
  32.7 10.6 %all_to_all.31.parts = f32[8,32,128]{2,1,0:T(8,128)S(1)} all-to-all(f32[8,32,128]{2,1,0:T(8,128)S(1)} %broadcast_in_dim.2), channel_id=1, replica_groups=mesh['x'=4,'h'=8,'l'=2,'y'=4,'c'=2] {'x','l'}, dimensions={0} | all-to-all | bytes 262144 | tf_op jit(solution)/shard_map/all_to_all | solution.py:38
  43.3 0.5 shard_map.77
  43.8 6.2 %collective-permute-start = (f32[64,1152]{1,0:T(8,128)S(1)}, f32[64,1152]{1,0:T(8,128)S(1)}, u32[]{:S(2)}, u32[]{:S(2)}) collective-permute-start(f32[64,1152]{1,0:T(8,128)S(1)} %get-tuple-element.31), channel_id=1, source_target_pairs={{0,1},{1,0},{2,3},{3,2},{4,5},{5,4},{6,7},{7,6},{8,9},{9,8},{10,11... | collective-permute-start | bytes 884744 | tf_op jit(solution)/shard_map/ppermute | solution.py:42
  50.0 0.5 shard_map.78
  50.5 0.7 collective-permute-done.other
  51.2 13.3 %all_to_all.32.parts = f32[32,2,1152]{2,1,0:T(2,128)S(1)} all-to-all(f32[32,2,1152]{2,1,0:T(2,128)S(1)} %shard_map.79), channel_id=1, replica_groups=mesh['x'=4,'h'=8,'l'=2,'y'=4,'c'=2] {'x','l','y'}, dimensions={0} | all-to-all | bytes 589824 | tf_op jit(solution)/shard_map/all_to_all | solution.py:38
  64.6 14.7 %all_to_all.33.parts = f32[8,2,1152]{2,1,0:T(2,128)S(1)} all-to-all(f32[8,2,1152]{2,1,0:T(2,128)S(1)} %shard_map.80), channel_id=1, replica_groups=mesh['x'=4,'h'=8,'l'=2,'y'=4,'c'=2] {'h'}, dimensions={0} | all-to-all | bytes 147456 | tf_op jit(solution)/shard_map/all_to_all | solution.py:38
  79.3 0.2 shard_map.81
  79.5 11.8 %all_to_all.34.parts = f32[32,2,1024]{2,1,0:T(2,128)S(1)} all-to-all(f32[32,2,1024]{2,1,0:T(2,128)S(1)} %shard_map.81), channel_id=1, replica_groups=mesh['x'=4,'h'=8,'l'=2,'y'=4,'c'=2] {'x','l','y'}, dimensions={0} | all-to-all | bytes 524288 | tf_op jit(solution)/shard_map/all_to_all | solution.py:38
  91.4 6.5 %collective-permute-start.1 = (f32[32,2,1024]{2,1,0:T(2,128)S(1)}, f32[32,2,1024]{2,1,0:T(2,128)S(1)}, u32[]{:S(2)}, u32[]{:S(2)}) collective-permute-start(f32[32,2,1024]{2,1,0:T(2,128)S(1)} %all_to_all.34.parts), channel_id=1, source_target_pairs={{0,1},{1,0},{2,3},{3,2},{4,5},{5,4},{6,7},{7,6},{8,9},{9,8},{10,11... | collective-permute-start | bytes 786440 | tf_op jit(solution)/shard_map/ppermute | solution.py:42
  97.9 0.3 shard_map.82
  98.2 0.8 collective-permute-done.1.parts
  99.0 1.0 shard_map.83
  100.0 8.2 %all_to_all.35.parts = f32[8,32,128]{2,1,0:T(8,128)S(1)} all-to-all(f32[8,32,128]{2,1,0:T(8,128)S(1)} %get-tuple-element.38), channel_id=1, replica_groups=mesh['x'=4,'h'=8,'l'=2,'y'=4,'c'=2] {'y','c'}, dimensions={0} | all-to-all | bytes 262144 | tf_op jit(solution)/shard_map/all_to_all | solution.py:38
  108.2 0.8 shard_map.84
  (4 shorter events, 0.1 us)
Async XLA Ops:
  43.8 7.4 %collective-permute-start = (f32[64,1152]{1,0:T(8,128)S(1)}, f32[64,1152]{1,0:T(8,128)S(1)}, u32[]{:S(2)}, u32[]{:S(2)}) collective-permute-start(f32[64,1152]{1,0:T(8,128)S(1)} %get-tuple-element.31), channel_id=1, source_target_pairs={{0,1},{1,0},{2,3},{3,2},{4,5},{5,4},{6,7},{7,6},{8,9},{9,8},{10,11... | collective-permute-start | bytes 884744 | tf_op jit(solution)/shard_map/ppermute | solution.py:42
  91.4 7.6 %collective-permute-start.1 = (f32[32,2,1024]{2,1,0:T(2,128)S(1)}, f32[32,2,1024]{2,1,0:T(2,128)S(1)}, u32[]{:S(2)}, u32[]{:S(2)}) collective-permute-start(f32[32,2,1024]{2,1,0:T(2,128)S(1)} %all_to_all.34.parts), channel_id=1, source_target_pairs={{0,1},{1,0},{2,3},{3,2},{4,5},{5,4},{6,7},{7,6},{8,9},{9,8},{10,11... | collective-permute-start | bytes 786440 | tf_op jit(solution)/shard_map/ppermute | solution.py:42

commit v10 on v8

--- a/solution.py
+++ b/solution.py
@@ -53,22 +53,31 @@
     far, count = refs[:3], refs[3]
     runs_out, gram_out, empty, low, below, *near, sems = refs[4:]
     bins, run_init, times = near
-    copies = [pltpu.make_async_copy(far[i], near[i], sems.at[i]) for i in range(3)]
-    for copy in reversed(copies):
+    middle = bins.shape[0] // 2
+    halves = [pl.ds(i * middle, middle) for i in range(2)]
+    small = [pltpu.make_async_copy(far[i], near[i], sems.at[i]) for i in (1, 2)]
+    large = [
+        pltpu.make_async_copy(far[0].at[part], bins.at[part], sems.at[3 * i])
+        for i, part in enumerate(halves)
+    ]
+    for copy in (*large, *small):
         copy.start()
     slot = lax.broadcasted_iota(jnp.int32, run_init.shape, 0)
-    copies[1].wait()
+    small[0].wait()
     live = slot < count[0]
     empty[...] = jnp.where(live, 0.0, 1.0)
     runs = jnp.where(live, run_init[...], 0.0)
     runs_out[...] = runs
     run_gram = exact(runs, runs, FIRST)
     gram_out[...] = run_gram
-    copies[2].wait()
-    copies[0].wait()
-    full = bins[...]
-    low[...] = full.astype(BF16)
-    below[...] = jnp.dot(times[...], run_gram * square(full, FIRST), precision=HIGH)
+    small[1].wait()
+    grams = []
+    for copy, part in zip(large, halves):
+        copy.wait()
+        full = bins[part]
+        low[part] = full.astype(BF16)
+        grams.append(square(full, FIRST))
+    below[...] = jnp.dot(times[...], run_gram * (grams[0] + grams[1]), precision=HIGH)
 
 
 def terms_kernel(tensor, low, runs, below, both):
@@ -262,7 +271,7 @@
             shape_of((rows, rank)),
         ),
         [pl.BlockSpec(memory_space=space) for space in (*[pl.ANY] * 3, pltpu.SMEM)],
-        scratch_shapes=[pltpu.SemaphoreType.DMA((3,))],
+        scratch_shapes=[pltpu.SemaphoreType.DMA((4,))],
     )
     shape = (extent(NEAR), 2 * rows, rank)
     (both,) = local(terms_kernel, (flat, low, runs, below), [shape_of(shape)])

time: 108 us -> 108 us (level)
  no operation moved by 1% of the time
where the time goes in v10:
time: 108 us
  blocking collectives  87.2 us (81%)
  starting transfers between devices  11.4 us (11%)
  Pallas kernels  6.19 us (6%)
  waiting for transfers between devices  1.53 us (1%)
  between operations  1.42 us (1%)
    all_to_all x6, blocking collectives, exchange(): return lax.all_to_all(parts, axes, 0, 0)  87.2 us
    ppermute x2, starting transfers between devices, swap(): return lax.ppermute(value, PAIR, [(0, 1), (1, 0)])  11.4 us
    pallas_call x10, Pallas kernels, local(): pl.pallas_call(kernel, out_shape=tuple(shapes), in_specs=specs or [near]...  6.19 us
  transfers between devices with their start and end apart: 2, of which 2 were waited for; matrix products, arithmetic and copies ran while one was open for 0% of the time, Pallas kernels for 1%

profile of v10, /device:TPU:1, one launch (start us, length us, event | category | flops | bytes accessed | tf_op | source)
XLA Modules:
  0.0 107.8 jit_solution(6922923476371866304)
XLA Ops:
  0.6 0.0 copy-start
  1.3 2.5 %shard_map.76 = (f32[16,128]{1,0:T(8,128)S(1)}, f32[128,128]{1,0:T(8,128)S(1)}, f32[16,128]{1,0:T(8,128)S(1)}, bf16[1024,128]{1,0:T(8,128)(2,1)S(1)}, f32[16,128...) custom-call(f32[1024,128]{1,0:T(8,128)} %refs_0_.1, f32[16,128]{1,0:T(8,128)} %refs_1_.1, ...), custom_call_target="tpu_custom_call" | custom-call | tf_op jit(solution)/shard_map/pallas_call | solution.py:241
  3.8 0.0 copy-done
  3.8 0.3 shard_map.77
  4.1 11.5 %all_to_all.30 = f32[8,32,128]{2,1,0:T(8,128)S(1)} all-to-all(f32[8,32,128]{2,1,0:T(8,128)S(1)} %shard_map.77), channel_id=1, replica_groups=mesh['x'=4,'h'=8,'l'=2,'y'=4,'c'=2] {'x','l'}, dimensions={0} | all-to-all | bytes 262144 | tf_op jit(solution)/shard_map/all_to_all | solution.py:38
  15.7 27.0 %all_to_all.31.parts = f32[8,32,128]{2,1,0:T(8,128)S(1)} all-to-all(f32[8,32,128]{2,1,0:T(8,128)S(1)} %broadcast_in_dim.2), channel_id=1, replica_groups=mesh['x'=4,'h'=8,'l'=2,'y'=4,'c'=2] {'h'}, dimensions={0} | all-to-all | bytes 262144 | tf_op jit(solution)/shard_map/all_to_all | solution.py:38
  42.7 0.5 shard_map.78
  43.2 4.9 %collective-permute-start = (f32[64,1152]{1,0:T(8,128)S(1)}, f32[64,1152]{1,0:T(8,128)S(1)}, u32[]{:S(2)}, u32[]{:S(2)}) collective-permute-start(f32[64,1152]{1,0:T(8,128)S(1)} %get-tuple-element.31), channel_id=1, source_target_pairs={{0,1},{1,0},{2,3},{3,2},{4,5},{5,4},{6,7},{7,6},{8,9},{9,8},{10,11... | collective-permute-start | bytes 884744 | tf_op jit(solution)/shard_map/ppermute | solution.py:42
  48.1 0.5 shard_map.79
  48.6 0.7 collective-permute-done.other
  49.3 13.7 %all_to_all.32.parts = f32[32,2,1152]{2,1,0:T(2,128)S(1)} all-to-all(f32[32,2,1152]{2,1,0:T(2,128)S(1)} %shard_map.80), channel_id=1, replica_groups=mesh['x'=4,'h'=8,'l'=2,'y'=4,'c'=2] {'x','l','y'}, dimensions={0} | all-to-all | bytes 589824 | tf_op jit(solution)/shard_map/all_to_all | solution.py:38
  63.0 14.9 %all_to_all.33.parts = f32[8,2,1152]{2,1,0:T(2,128)S(1)} all-to-all(f32[8,2,1152]{2,1,0:T(2,128)S(1)} %shard_map.81), channel_id=1, replica_groups=mesh['x'=4,'h'=8,'l'=2,'y'=4,'c'=2] {'h'}, dimensions={0} | all-to-all | bytes 147456 | tf_op jit(solution)/shard_map/all_to_all | solution.py:38
  77.9 0.2 shard_map.82
  78.2 11.9 %all_to_all.34.parts = f32[32,2,1024]{2,1,0:T(2,128)S(1)} all-to-all(f32[32,2,1024]{2,1,0:T(2,128)S(1)} %shard_map.82), channel_id=1, replica_groups=mesh['x'=4,'h'=8,'l'=2,'y'=4,'c'=2] {'x','l','y'}, dimensions={0} | all-to-all | bytes 524288 | tf_op jit(solution)/shard_map/all_to_all | solution.py:38
  90.1 6.6 %collective-permute-start.1 = (f32[32,2,1024]{2,1,0:T(2,128)S(1)}, f32[32,2,1024]{2,1,0:T(2,128)S(1)}, u32[]{:S(2)}, u32[]{:S(2)}) collective-permute-start(f32[32,2,1024]{2,1,0:T(2,128)S(1)} %all_to_all.34.parts), channel_id=1, source_target_pairs={{0,1},{1,0},{2,3},{3,2},{4,5},{5,4},{6,7},{7,6},{8,9},{9,8},{10,11... | collective-permute-start | bytes 786440 | tf_op jit(solution)/shard_map/ppermute | solution.py:42
  96.7 0.3 shard_map.83
  97.0 0.8 collective-permute-done.1.parts
  97.8 1.0 shard_map.84
  98.8 8.2 %all_to_all.35.parts = f32[8,32,128]{2,1,0:T(8,128)S(1)} all-to-all(f32[8,32,128]{2,1,0:T(8,128)S(1)} %get-tuple-element.38), channel_id=1, replica_groups=mesh['x'=4,'h'=8,'l'=2,'y'=4,'c'=2] {'y','c'}, dimensions={0} | all-to-all | bytes 262144 | tf_op jit(solution)/shard_map/all_to_all | solution.py:38
  107.0 0.8 shard_map.85
  (4 shorter events, 0.1 us)
Async XLA Ops:
  0.6 3.2 %copy-start = (bf16[16,16,1024]{2,1,0:T(8,128)(2,1)S(1)}, bf16[16,16,1024]{2,1,0:T(8,128)(2,1)}, u32[]{:S(2)}) copy-start(bf16[16,16,1024]{2,1,0:T(8,128)(2,1)} %param.5) | copy-start | bytes 1572868
  43.2 6.1 %collective-permute-start = (f32[64,1152]{1,0:T(8,128)S(1)}, f32[64,1152]{1,0:T(8,128)S(1)}, u32[]{:S(2)}, u32[]{:S(2)}) collective-permute-start(f32[64,1152]{1,0:T(8,128)S(1)} %get-tuple-element.31), channel_id=1, source_target_pairs={{0,1},{1,0},{2,3},{3,2},{4,5},{5,4},{6,7},{7,6},{8,9},{9,8},{10,11... | collective-permute-start | bytes 884744 | tf_op jit(solution)/shard_map/ppermute | solution.py:42
  90.1 7.7 %collective-permute-start.1 = (f32[32,2,1024]{2,1,0:T(2,128)S(1)}, f32[32,2,1024]{2,1,0:T(2,128)S(1)}, u32[]{:S(2)}, u32[]{:S(2)}) collective-permute-start(f32[32,2,1024]{2,1,0:T(2,128)S(1)} %all_to_all.34.parts), channel_id=1, source_target_pairs={{0,1},{1,0},{2,3},{3,2},{4,5},{5,4},{6,7},{7,6},{8,9},{9,8},{10,11... | collective-permute-start | bytes 786440 | tf_op jit(solution)/shard_map/ppermute | solution.py:42

commit v11 on v7

--- a/solution.py
+++ b/solution.py
@@ -68,7 +68,7 @@
     gram_out[...] = run_gram
     copies[1].wait()
     full = bins[...]
-    below = jnp.dot(times[...], run_gram * exact(full, full, FIRST), precision=HIGH)
+    below = jnp.dot(times[...], run_gram * square(full, FIRST), precision=HIGH)
     copies[0].wait()
     inner = jnp.dot(tensor[...], full.astype(BF16), preferred_element_type=F32)
     terms = runs[0:1] * inner[0:rows]
@@ -85,6 +85,13 @@
         out.append(value.astype(BF16))
         value = value - out[-1].astype(F32)
     return out
+
+
+def square(value, dims):
+    high, mid, low = pieces(value)
+    cross = quick(high, mid, dims)
+    far = quick(high, low, dims)
+    return quick(high, high, dims) + (cross + cross.T) + (quick(mid, mid, dims) + far + far.T)
 
 
 def half_terms(runs, times, tensor, side):

time: 108 us -> 108 us (level)
  no operation moved by 1% of the time
where the time goes in v11:
time: 108 us
  blocking collectives  87.2 us (81%)
  starting transfers between devices  11.4 us (11%)
  Pallas kernels  6.02 us (6%)
  waiting for transfers between devices  1.53 us (1%)
  between operations  1.34 us (1%)
    all_to_all x6, blocking collectives, exchange(): return lax.all_to_all(parts, axes, 0, 0)  87.2 us
    ppermute x2, starting transfers between devices, swap(): return lax.ppermute(value, PAIR, [(0, 1), (1, 0)])  11.4 us
    pallas_call x9, Pallas kernels, local(): pl.pallas_call(kernel, out_shape=tuple(shapes), in_specs=specs or [near]...  6.02 us
  transfers between devices with their start and end apart: 2, of which 2 were waited for; matrix products, arithmetic and copies ran while one was open for 0% of the time, Pallas kernels for 1%

profile of v11, /device:TPU:1, one launch (start us, length us, event | category | flops | bytes accessed | tf_op | source)
XLA Modules:
  0.0 107.6 jit_solution(10052609550989399229)
XLA Ops:
  1.3 2.6 %shard_map.76 = (f32[8,32,128]{2,1,0:T(8,128)S(1)}, f32[16,128]{1,0:T(8,128)S(1)}, f32[128,128]{1,0:T(8,128)S(1)}, f32[16,128]{1,0:T(8,128)S(1)}, bf16[256,1024]...) custom-call(bf16[256,1024]{1,0:T(8,128)(2,1)} %bitcast.1, ...), custom_call_target="tpu_custom_call" | custom-call | tf_op jit(solution)/shard_map/pallas_call | solution.py:228
  3.9 11.5 %all_to_all.30 = f32[8,32,128]{2,1,0:T(8,128)S(1)} all-to-all(f32[8,32,128]{2,1,0:T(8,128)S(1)} %get-tuple-element.23), channel_id=1, replica_groups=mesh['x'=4,'h'=8,'l'=2,'y'=4,'c'=2] {'x','l'}, dimensions={0} | all-to-all | bytes 262144 | tf_op jit(solution)/shard_map/all_to_all | solution.py:38
  15.4 27.0 %all_to_all.31.parts = f32[8,32,128]{2,1,0:T(8,128)S(1)} all-to-all(f32[8,32,128]{2,1,0:T(8,128)S(1)} %broadcast_in_dim.2), channel_id=1, replica_groups=mesh['x'=4,'h'=8,'l'=2,'y'=4,'c'=2] {'h'}, dimensions={0} | all-to-all | bytes 262144 | tf_op jit(solution)/shard_map/all_to_all | solution.py:38
  42.4 0.5 shard_map.77
  42.9 4.9 %collective-permute-start = (f32[64,1152]{1,0:T(8,128)S(1)}, f32[64,1152]{1,0:T(8,128)S(1)}, u32[]{:S(2)}, u32[]{:S(2)}) collective-permute-start(f32[64,1152]{1,0:T(8,128)S(1)} %get-tuple-element.31), channel_id=1, source_target_pairs={{0,1},{1,0},{2,3},{3,2},{4,5},{5,4},{6,7},{7,6},{8,9},{9,8},{10,11... | collective-permute-start | bytes 884744 | tf_op jit(solution)/shard_map/ppermute | solution.py:42
  47.8 0.5 shard_map.78
  48.3 0.7 collective-permute-done.other
  49.0 13.7 %all_to_all.32.parts = f32[32,2,1152]{2,1,0:T(2,128)S(1)} all-to-all(f32[32,2,1152]{2,1,0:T(2,128)S(1)} %shard_map.79), channel_id=1, replica_groups=mesh['x'=4,'h'=8,'l'=2,'y'=4,'c'=2] {'x','l','y'}, dimensions={0} | all-to-all | bytes 589824 | tf_op jit(solution)/shard_map/all_to_all | solution.py:38
  62.8 14.9 %all_to_all.33.parts = f32[8,2,1152]{2,1,0:T(2,128)S(1)} all-to-all(f32[8,2,1152]{2,1,0:T(2,128)S(1)} %shard_map.80), channel_id=1, replica_groups=mesh['x'=4,'h'=8,'l'=2,'y'=4,'c'=2] {'h'}, dimensions={0} | all-to-all | bytes 147456 | tf_op jit(solution)/shard_map/all_to_all | solution.py:38
  77.7 0.2 shard_map.81
  77.9 11.9 %all_to_all.34.parts = f32[32,2,1024]{2,1,0:T(2,128)S(1)} all-to-all(f32[32,2,1024]{2,1,0:T(2,128)S(1)} %shard_map.81), channel_id=1, replica_groups=mesh['x'=4,'h'=8,'l'=2,'y'=4,'c'=2] {'x','l','y'}, dimensions={0} | all-to-all | bytes 524288 | tf_op jit(solution)/shard_map/all_to_all | solution.py:38
  89.8 6.6 %collective-permute-start.1 = (f32[32,2,1024]{2,1,0:T(2,128)S(1)}, f32[32,2,1024]{2,1,0:T(2,128)S(1)}, u32[]{:S(2)}, u32[]{:S(2)}) collective-permute-start(f32[32,2,1024]{2,1,0:T(2,128)S(1)} %all_to_all.34.parts), channel_id=1, source_target_pairs={{0,1},{1,0},{2,3},{3,2},{4,5},{5,4},{6,7},{7,6},{8,9},{9,8},{10,11... | collective-permute-start | bytes 786440 | tf_op jit(solution)/shard_map/ppermute | solution.py:42
  96.4 0.3 shard_map.82
  96.7 0.8 collective-permute-done.1.parts
  97.6 1.0 shard_map.83
  98.5 8.2 %all_to_all.35.parts = f32[8,32,128]{2,1,0:T(8,128)S(1)} all-to-all(f32[8,32,128]{2,1,0:T(8,128)S(1)} %get-tuple-element.38), channel_id=1, replica_groups=mesh['x'=4,'h'=8,'l'=2,'y'=4,'c'=2] {'y','c'}, dimensions={0} | all-to-all | bytes 262144 | tf_op jit(solution)/shard_map/all_to_all | solution.py:38
  106.7 0.8 shard_map.84
  (4 shorter events, 0.1 us)
Async XLA Ops:
  42.9 6.1 %collective-permute-start = (f32[64,1152]{1,0:T(8,128)S(1)}, f32[64,1152]{1,0:T(8,128)S(1)}, u32[]{:S(2)}, u32[]{:S(2)}) collective-permute-start(f32[64,1152]{1,0:T(8,128)S(1)} %get-tuple-element.31), channel_id=1, source_target_pairs={{0,1},{1,0},{2,3},{3,2},{4,5},{5,4},{6,7},{7,6},{8,9},{9,8},{10,11... | collective-permute-start | bytes 884744 | tf_op jit(solution)/shard_map/ppermute | solution.py:42
  89.8 7.7 %collective-permute-start.1 = (f32[32,2,1024]{2,1,0:T(2,128)S(1)}, f32[32,2,1024]{2,1,0:T(2,128)S(1)}, u32[]{:S(2)}, u32[]{:S(2)}) collective-permute-start(f32[32,2,1024]{2,1,0:T(2,128)S(1)} %all_to_all.34.parts), channel_id=1, source_target_pairs={{0,1},{1,0},{2,3},{3,2},{4,5},{5,4},{6,7},{7,6},{8,9},{9,8},{10,11... | collective-permute-start | bytes 786440 | tf_op jit(solution)/shard_map/ppermute | solution.py:42
